TPU v7x, 32 devices: a whole 2x2x4 slice. The times are simulated.
32 devices in a mesh: seq: 4 (over x, core), fsdp: 8 (over z, y).
Axes of the slice: x: 2, y: 2, z: 4, core: 2. Of those that a mesh axis runs over, the one named last changes fastest.
Arguments:
- tokens: bfloat16 [64, 256, 512], P('fsdp', 'seq'), may hold values from -6 to 6
- pad_mask: int32 [64, 256], P('fsdp', 'seq'), may hold values from 0 to 1, as said below
- routes: int32 [64, 256, 2], P('fsdp', 'seq'), may hold values from 0 to 3, all different within a row
- ln1_gain: float32 [512], P('fsdp'), may hold values from 0.5 to 1.5
- w_qkv: float32 [512, 1536], P('fsdp'), may hold values from -0.25 to 0.25
- w_proj: float32 [512, 512], P('fsdp'), may hold values from -1 to 1
- ln2_gain: float32 [512], P('fsdp'), may hold values from 0.5 to 1.5
- w_router: float32 [512, 4], P('fsdp'), may hold values from -0.1875 to 0.1875
- exp_in: float32 [2048, 4, 512], P('fsdp'), may hold values from -0.25 to 0.25
- exp_out: float32 [2048, 4, 512], P('fsdp'), may hold values from -0.375 to 0.375
- cotangent: bfloat16 [64, 256, 512], P('fsdp', 'seq'), may hold values from -6 to 6
Outputs:
- block_out: bfloat16 [64, 256, 512], P('fsdp', 'seq')
- grad_tokens: float32 [64, 256, 512], P('fsdp', 'seq')
- grad_ln1_gain: float32 [512], P('fsdp')
- grad_w_qkv: float32 [512, 1536], P('fsdp')
- grad_w_proj: float32 [512, 512], P('fsdp')
- grad_ln2_gain: float32 [512], P('fsdp')
- grad_w_router: float32 [512, 4], P('fsdp')
- grad_exp_in: float32 [2048, 4, 512], P('fsdp')
- grad_exp_out: float32 [2048, 4, 512], P('fsdp')
Inputs may be any that keep to these rules, and one draw needn't show every extreme that they name: pad_mask is 1 on the first tokens of each image and 0 after them; at least 192 tokens of every image are real, and image 0 has all 256. `routes`: the two experts of a token differ.
All inputs are finite; a program needn't handle non-finite values.
Results may differ from a plain program's by a relative error of at most 0.014.
Values may be sent and summed in bfloat16 or wider, within the bound.
No kernel may reach another device: no remote copies, remote signals or barrier semaphores. Data moves between devices by JAX's collectives and lax.ppermute only.
A program may use at most 320 MiB of HBM per device.

v0:
```python
import jax
import jax.numpy as jnp
from jax import lax
from jax.experimental import pallas as pl
from jax.experimental.pallas import tpu as pltpu
from jax.sharding import PartitionSpec as P

BF = jnp.bfloat16
F32 = jnp.float32
HEADS = 8
HEAD = 64
EPS = 1e-06
SQRT_HALF = 0.7071067811865476
INV_ROOT_TWO_PI = 0.3989422804014327
SMALL = 256
CODE_ROWS = 16
NT = (((1,), (1,)), ((), ()))
TN = (((0,), (0,)), ((), ()))
MIB = 1 << 20
PACE = 0.0001


def cost(us):
    return pl.CostEstimate(
        flops=int(us * 1.15e9 * PACE) + 1, bytes_accessed=int(us * 1e5 * PACE) + 1, transcendentals=0
    )


def dot(a, b, dims=(((1,), (0,)), ((), ()))):
    return lax.dot_general(a, b, dims, preferred_element_type=F32)


def ring_order(n):
    return [2 * i for i in range(n // 2)] + [2 * i + 1 for i in reversed(range(n // 2))]


def ring_pairs(orders):
    fw = []
    for order in orders:
        n = len(order)
        fw += [(order[i], order[(i + 1) % n]) for i in range(n)]
    return fw, [(b, a) for a, b in fw]


def send(x, axis, pairs):
    return lax.ppermute(x, axis, pairs)


def add_low(a, b):
    return (a.astype(F32) + b.astype(F32)).astype(BF)


def norm(v):
    c = v - jnp.mean(v, axis=-1, keepdims=True)
    inv = lax.rsqrt(jnp.mean(c * c, axis=-1, keepdims=True) + EPS)
    return c * inv, inv


def norm_back(u, hat, inv):
    return inv * (
        u
        - jnp.mean(u, axis=-1, keepdims=True)
        - hat * jnp.mean(u * hat, axis=-1, keepdims=True)
    )


def block_kernel(own_ref, qkv_ref, proj_ref, small_ref, out_ref):
    mid = out_ref.shape[1]
    rest = qkv_ref.shape[1] - mid
    width = proj_ref.shape[1]

    @pl.when((own_ref[0] & 1) == 0)
    def _():
        out_ref[...] = qkv_ref[:, :mid].astype(BF)

    @pl.when((own_ref[0] & 1) == 1)
    def _():
        out_ref[:, :rest] = qkv_ref[:, mid:].astype(BF)
        out_ref[:, rest : rest + width] = proj_ref[...].astype(BF)
        out_ref[:, rest + width :] = small_ref[...].astype(BF)


def block_of(own, w_qkv, w_proj, small):
    rows = w_qkv.shape[0]
    mid = (w_qkv.shape[1] + w_proj.shape[1] + SMALL) // 2
    whole = pl.BlockSpec(memory_space=pltpu.VMEM)
    return pl.pallas_call(
        block_kernel,
        in_specs=[pl.BlockSpec(memory_space=pltpu.SMEM)] + [whole] * 3,
        out_specs=whole,
        out_shape=jax.ShapeDtypeStruct((rows, mid), BF),
        compiler_params=pltpu.CompilerParams(vmem_limit_bytes=8 * MIB),
        cost_estimate=cost(1),
    )(own, w_qkv, w_proj, small)


def unpack_kernel(own_ref, p0, p1, p2, p3, tok_ref, code_ref, cot_ref):
    own = own_ref[0]
    seg, width = tok_ref.shape[2:]
    for r, piece in enumerate((p0, p1, p2, p3)):
        at = own ^ r
        tok_ref[at, 0] = piece[0, :, :width]
        code_ref[at, 0] = piece[0, :, 2 * width :]
        cot_ref[0, pl.ds(pl.multiple_of(at * seg, seg), seg)] = piece[0, :, width : 2 * width]

    seq_len = 4 * seg
    code = code_ref[:, 0].astype(F32).reshape(seq_len, 128).T
    cot_ref[0, seq_len:, :seq_len] = code[:CODE_ROWS].astype(BF)
    cot_ref[0, seq_len:, seq_len:] = jnp.zeros((CODE_ROWS, width - seq_len), BF)


def unpack(own, pieces, width):
    images, seg, cols = pieces[0].shape
    rows = 4 * seg + CODE_ROWS
    piece = pl.BlockSpec((1, seg, cols), lambda i: (i, 0, 0))
    nat = lambda w: pl.BlockSpec((4, 1, seg, w), lambda i: (0, i, 0, 0))
    shape = lambda *d: jax.ShapeDtypeStruct(d, BF)
    return pl.pallas_call(
        unpack_kernel,
        grid=(images,),
        in_specs=[pl.BlockSpec(memory_space=pltpu.SMEM)] + [piece] * 4,
        out_specs=[nat(width), nat(128), pl.BlockSpec((1, rows, width), lambda i: (i, 0, 0))],
        out_shape=[
            shape(4, images, seg, width),
            shape(4, images, seg, 128),
            shape(images, rows, width),
        ],
        compiler_params=pltpu.CompilerParams(vmem_limit_bytes=8 * MIB),
        cost_estimate=cost(1.5),
    )(own, *pieces)


def gather_kernel(n_pieces, offs, *refs):
    pieces, out_ref, sems = refs[:n_pieces], refs[n_pieces], refs[n_pieces + 1]
    copies, k = [], 0
    for piece in pieces:
        for part in range(piece.shape[0]):
            rows = piece.shape[1]
            off = pl.multiple_of(offs[k], rows)
            copies.append(
                pltpu.make_async_copy(piece.at[part], out_ref.at[pl.ds(off, rows)], sems.at[k])
            )
            k += 1
    for copy in copies:
        copy.start()
    for copy in copies:
        copy.wait()


def gather_rows(pieces, offs, shape):
    n = len(pieces)
    anywhere = pl.BlockSpec(memory_space=pl.ANY)
    return pl.pallas_call(
        lambda *a: gather_kernel(n, *a),
        in_specs=[pl.BlockSpec(memory_space=pltpu.SMEM)] + [anywhere] * n,
        out_specs=pl.BlockSpec(memory_space=pltpu.VMEM),
        out_shape=jax.ShapeDtypeStruct(shape, BF),
        scratch_shapes=[pltpu.SemaphoreType.DMA((sum(p.shape[0] for p in pieces),))],
        compiler_params=pltpu.CompilerParams(vmem_limit_bytes=8 * MIB),
        cost_estimate=cost(2),
    )(offs, *pieces)


def attn_fwd_kernel(own_ref, tok_ref, code_ref, mine_ref, other_ref, *refs):
    n2a_ref, n2b_ref, res_ref, qkv_ref, ctx_ref, w_ref, gain_ref, wr_ref = refs
    img = pl.program_id(0)
    seq_len, width = res_ref.shape[1:]
    mid = mine_ref.shape[1]
    own = own_ref[0]

    @pl.when(img == 0)
    def _():
        for core, left, right in ((0, mine_ref, other_ref), (1, other_ref, mine_ref)):

            @pl.when((own & 1) == core)
            def _():
                w_ref[:, :mid] = left[...]
                w_ref[:, mid:] = right[...]

        small = w_ref[:, 4 * width : 4 * width + 128].astype(F32).T
        gain_ref[...] = small[0:16]
        for r in range(4):
            wr_ref[r : r + 1] = gain_ref[pl.ds(8 + (own ^ r), 1)]
        wr_ref[4:8] = jnp.zeros((4, width), F32)

    code = code_ref[:, 0].reshape(seq_len, 128).astype(F32)
    keep = (code[:, 0:1].astype(jnp.int32) & 1) > 0
    key_ok = (code.T[0:1].astype(jnp.int32) & 1) > 0
    x = tok_ref[:, 0].reshape(seq_len, width).astype(F32)
    hat, _ = norm(x)
    n1 = (hat * gain_ref[0:1]).astype(BF)
    qkv_ref[0] = dot(n1, w_ref[:, : 3 * width]).astype(BF)
    parts = []
    for h in range(HEADS):
        q = qkv_ref[0, :, h * HEAD : (h + 1) * HEAD]
        k = qkv_ref[0, :, width + h * HEAD : width + (h + 1) * HEAD]
        v = qkv_ref[0, :, 2 * width + h * HEAD : 2 * width + (h + 1) * HEAD]
        s = jnp.where(key_ok, dot(q, k, NT) * 0.125, -1e30)
        e = jnp.exp(s - jnp.max(s, axis=-1, keepdims=True))
        p = (e * (1.0 / jnp.sum(e, axis=-1, keepdims=True))).astype(BF)
        parts.append(dot(p, v))
    ctx = jnp.concatenate(parts, axis=1).astype(BF)
    ctx_ref[0] = ctx
    res = x + jnp.where(keep, dot(ctx, w_ref[:, 3 * width : 4 * width]), 0.0)
    res_ref[0] = res
    hat2, _ = norm(res)
    n2 = (hat2 * gain_ref[1:2]).astype(BF)
    half = pl.num_programs(0) // 2
    for k, ref in ((0, n2a_ref), (1, n2b_ref)):

        @pl.when((img >= k * half) & (img < (k + 1) * half))
        def _():
            ref[0] = n2


def attn_fwd(own, tok, code, mine, other):
    parts, images, seg, width = tok.shape
    seq_len, half = parts * seg, images // 2
    row = lambda w: pl.BlockSpec((1, seq_len, w), lambda i, *_: (i, 0, 0))
    whole = lambda s: pl.BlockSpec(s, lambda i, *_: (0,) * len(s))
    side = lambda k: pl.BlockSpec(
        (1, seq_len, width), lambda i, *_: (jnp.clip(i - k * half, 0, half - 1), 0, 0)
    )
    cols = 4 * width + SMALL
    return pl.pallas_call(
        attn_fwd_kernel,
        grid_spec=pltpu.PrefetchScalarGridSpec(
            num_scalar_prefetch=1,
            grid=(images,),
            in_specs=[
                pl.BlockSpec((parts, 1, seg, width), lambda i, *_: (0, i, 0, 0)),
                pl.BlockSpec((parts, 1, seg, 128), lambda i, *_: (0, i, 0, 0)),
                whole(mine.shape),
                whole(other.shape),
            ],
            out_specs=[
                side(0),
                side(1),
                row(width),
                row(3 * width),
                row(width),
                whole((width, cols)),
                whole((16, width)),
                whole((8, width)),
            ],
        ),
        out_shape=[
            jax.ShapeDtypeStruct((half, seq_len, width), BF),
            jax.ShapeDtypeStruct((half, seq_len, width), BF),
            jax.ShapeDtypeStruct((images, seq_len, width), F32),
            jax.ShapeDtypeStruct((images, seq_len, 3 * width), BF),
            jax.ShapeDtypeStruct((images, seq_len, width), BF),
            jax.ShapeDtypeStruct((width, cols), BF),
            jax.ShapeDtypeStruct((16, width), F32),
            jax.ShapeDtypeStruct((8, width), F32),
        ],
        compiler_params=pltpu.CompilerParams(vmem_limit_bytes=20 * MIB),
        cost_estimate=cost(8),
    )(own, tok, code, mine, other)


def router(own, n2, wr, code):
    ids = lax.broadcasted_iota(jnp.int32, (8, n2.shape[0]), 0)
    logits = jnp.where(ids < 4, dot(wr.astype(BF), n2, NT), -1e30)
    e = jnp.exp(logits - jnp.max(logits, axis=0, keepdims=True))
    probs = e * (1.0 / jnp.sum(e, axis=0, keepdims=True))
    route = code.astype(F32).astype(jnp.int32)
    first = (route >> 1) & 3
    second = route >> 3
    ids = ids ^ own
    chosen = ((ids == first) | (ids == second)).astype(F32)
    return probs, chosen


def weights_kernel(own_ref, *refs):
    win_ref, wout_ref = refs[:2]
    pieces = refs[2:-4]
    parts = len(pieces) // 4
    all_in, all_out, in_t, out_t = refs[-4:]
    own = own_ref[0]
    rows = win_ref.shape[1]
    for b in range(8):
        sl = slice(b * rows, (b + 1) * rows)
        if b < 4:
            a, c = win_ref[own ^ b], wout_ref[own ^ b]
        else:
            mine = pieces[(b - 4) * parts : (b - 3) * parts]
            a, c = (jnp.concatenate([p[k] for p in mine], axis=0) for k in range(2))
        all_in[sl] = a
        all_out[sl] = c
        in_t[:, sl] = a.T
        out_t[:, sl] = c.T


def weights(own, win, wout, pieces):
    rows, width = win.shape[1:]
    whole = pl.BlockSpec(memory_space=pltpu.VMEM)
    flat = jax.ShapeDtypeStruct((8 * rows, width), BF)
    turned = jax.ShapeDtypeStruct((width, 8 * rows), BF)
    return pl.pallas_call(
        weights_kernel,
        in_specs=[pl.BlockSpec(memory_space=pltpu.SMEM)] + [whole] * (2 + len(pieces)),
        out_specs=[whole] * 4,
        out_shape=[flat, flat, turned, turned],
        compiler_params=pltpu.CompilerParams(vmem_limit_bytes=16 * MIB),
        cost_estimate=cost(3),
    )(own, win, wout, *pieces)


def moe_kernel(starts, n_aliased, own_ref, wr_ref, win_ref, wout_ref, wint_ref, *refs):
    n = len(starts)
    xs, gs = refs[:n], refs[n : 2 * n]
    refs = refs[2 * n + n_aliased :]
    dx_refs = refs[:n]
    ga_ref, hg_ref, xo_ref, go_ref = refs[n:]
    step = pl.program_id(0)
    seq_len, width = xo_ref.shape[1:]
    rows = win_ref.shape[0] // 8
    within = []
    for j in range(n):
        low, high = starts[j], starts[j + 1] if j + 1 < n else None
        within.append((step >= low) if high is None else ((step >= low) & (step < high)))

        @pl.when(within[j])
        def _():
            xo_ref[0] = xs[j][0]
            go_ref[0] = gs[j][0]

    x = xo_ref[0]
    g = go_ref[0, :seq_len]
    probs, chosen = router(own_ref[0], x, wr_ref[...], go_ref[0, seq_len : seq_len + 1, :seq_len])
    gate = probs * chosen
    sums = [None] * 4
    for b in range(8):
        e = b % 4
        sl = slice(b * rows, (b + 1) * rows)
        h = dot(win_ref[sl], x, NT)
        u = dot(wout_ref[sl], g, NT)
        cumul = 0.5 * (1.0 + lax.erf(h * SQRT_HALF))
        slope = cumul + h * (INV_ROOT_TWO_PI * jnp.exp(-0.5 * h * h))
        act = h * cumul
        row = gate[e : e + 1]
        ga_ref[0, sl] = (act * row).astype(BF)
        hg_ref[0, sl] = (u * row * slope).astype(BF)
        part = jnp.sum(act * u, axis=0, keepdims=True)
        sums[e] = part if sums[e] is None else sums[e] + part
    dx = dot(wint_ref[...], hg_ref[0]).astype(BF)
    pad = jnp.zeros((CODE_ROWS - 4, seq_len), F32)
    tail = jnp.concatenate(sums + [pad], axis=0).astype(BF)
    for j in range(n):

        @pl.when(within[j])
        def _():
            dx_refs[j][0, :width] = dx
            dx_refs[j][0, width:] = tail


def moe_call(xs, gs, own, wr, win, wout, wint, first, units, bufs):
    n = len(xs)
    counts = [x.shape[0] for x in xs]
    starts = [sum(counts[:j]) for j in range(n)]
    total = sum(counts)
    seq_len, width = xs[0].shape[1:]
    f = win.shape[0]
    g_rows = gs[0][0].shape[1]

    def item(rows, j, at=0):
        lo, c = starts[j], counts[j]
        return pl.BlockSpec(
            (1, rows, width), lambda i: (at + jnp.clip(i - lo, 0, c - 1), 0, 0)
        )

    def out_item(j):
        lo, c = starts[j], counts[j]
        return pl.BlockSpec(
            (1, width + CODE_ROWS, seq_len), lambda i: (jnp.clip(i - lo, 0, c - 1), 0, 0)
        )

    whole = lambda s: pl.BlockSpec(s, lambda i: (0, 0), pipeline_mode=pl.Buffered(1))
    buf = lambda r, w: pl.BlockSpec((1, r, w), lambda i: (first + i, 0, 0))
    aliased = [] if bufs is None else list(bufs)
    base = 5 + 2 * n
    return pl.pallas_call(
        lambda *a: moe_kernel(starts, len(aliased), *a),
        grid=(total,),
        in_specs=[pl.BlockSpec(memory_space=pltpu.SMEM)]
        + [whole(wr.shape), whole(win.shape), whole(wout.shape), whole(wint.shape)]
        + [item(seq_len, j) for j in range(n)]
        + [item(g_rows, j, gs[j][1]) for j in range(n)]
        + [pl.BlockSpec(memory_space=pl.ANY)] * len(aliased),
        out_specs=[out_item(j) for j in range(n)]
        + [
            buf(f, seq_len),
            buf(f, seq_len),
            buf(seq_len, width),
            buf(g_rows, width),
        ],
        out_shape=[
            jax.ShapeDtypeStruct((c, width + CODE_ROWS, seq_len), BF) for c in counts
        ]
        + [
            jax.ShapeDtypeStruct((units, f, seq_len), BF),
            jax.ShapeDtypeStruct((units, f, seq_len), BF),
            jax.ShapeDtypeStruct((units, seq_len, width), BF),
            jax.ShapeDtypeStruct((units, g_rows, width), BF),
        ],
        input_output_aliases={base + k: n + k for k in range(len(aliased))},
        compiler_params=pltpu.CompilerParams(vmem_limit_bytes=16 * MIB),
        cost_estimate=cost(2.6 * total),
    )(own, wr, win, wout, wint, *xs, *[g for g, _ in gs], *aliased)


def moe_out_kernel(woutt_ref, ga_ref, out_ref):
    out_ref[0] = dot(woutt_ref[...], ga_ref[0]).astype(BF)


def moe_out(woutt, ga):
    units, f, seq_len = ga.shape
    width = woutt.shape[0]
    return pl.pallas_call(
        moe_out_kernel,
        grid=(units,),
        in_specs=[
            pl.BlockSpec((width, f), lambda i: (0, 0), pipeline_mode=pl.Buffered(1)),
            pl.BlockSpec((1, f, seq_len), lambda i: (i, 0, 0)),
        ],
        out_specs=pl.BlockSpec((1, width, seq_len), lambda i: (i, 0, 0)),
        out_shape=jax.ShapeDtypeStruct((units, width, seq_len), BF),
        compiler_params=pltpu.CompilerParams(vmem_limit_bytes=8 * MIB),
        cost_estimate=cost(0.7 * units),
    )(woutt, ga)


def moe_grad_kernel(groups, ga_ref, hg_ref, x_ref, g_ref, out_ref, acc_in, acc_out):
    seq_len = x_ref.shape[1]
    part = pl.program_id(1)
    a_in = a_out = None
    for u in range(x_ref.shape[0]):
        t_in = dot(hg_ref[u], x_ref[u])
        t_out = dot(ga_ref[u], g_ref[u, :seq_len])
        a_in = t_in if a_in is None else a_in + t_in
        a_out = t_out if a_out is None else a_out + t_out
    if groups == 1:
        out_ref[0, 0] = a_in.astype(BF)
        out_ref[0, 1] = a_out.astype(BF)
        return

    @pl.when(part == 0)
    def _():
        acc_in[...] = jnp.zeros_like(acc_in)
        acc_out[...] = jnp.zeros_like(acc_out)

    acc_in[...] += a_in
    acc_out[...] += a_out

    @pl.when(part == groups - 1)
    def _():
        out_ref[0, 0] = acc_in[...].astype(BF)
        out_ref[0, 1] = acc_out[...].astype(BF)


def moe_grad(ga, hg, xb, gb, r):
    units, f, seq_len = ga.shape
    width = xb.shape[2]
    rows = f // 8
    per = min(units, 8)
    groups = units // per
    act = pl.BlockSpec((per, rows, seq_len), lambda b, p: (p, 4 * b + r, 0))
    return pl.pallas_call(
        lambda *a: moe_grad_kernel(groups, *a),
        grid=(2, groups),
        in_specs=[
            act,
            act,
            pl.BlockSpec((per, seq_len, width), lambda b, p: (p, 0, 0)),
            pl.BlockSpec((per, gb.shape[1], width), lambda b, p: (p, 0, 0)),
        ],
        out_specs=pl.BlockSpec((1, 2, rows, width), lambda b, p: (b, 0, 0, 0)),
        out_shape=jax.ShapeDtypeStruct((2, 2, rows, width), BF),
        scratch_shapes=[pltpu.VMEM((rows, width), F32)] * 2,
        compiler_params=pltpu.CompilerParams(vmem_limit_bytes=15 * MIB),
        cost_estimate=cost(0.47 * units),
    )(ga, hg, xb, gb)


def pack_kernel(own_ref, *refs):
    pieces = refs[:4]
    in_ref, out_ref, held = refs[4:]
    for r in range(4):
        held[own_ref[0] ^ r] = pieces[r][...]
    for e in range(4):
        in_ref[:, e, :] = held[e, 0].astype(F32)
        out_ref[:, e, :] = held[e, 1].astype(F32)


def pack(own, pieces):
    rows, width = pieces[0].shape[1:]
    tile = min(rows, 64)
    piece = pl.BlockSpec((2, tile, width), lambda i: (0, i, 0))
    out = pl.BlockSpec((tile, 4, width), lambda i: (i, 0, 0))
    shape = jax.ShapeDtypeStruct((rows, 4, width), F32)
    return pl.pallas_call(
        pack_kernel,
        grid=(rows // tile,),
        in_specs=[pl.BlockSpec(memory_space=pltpu.SMEM)] + [piece] * 4,
        out_specs=[out, out],
        out_shape=[shape, shape],
        scratch_shapes=[pltpu.VMEM((4, 2, tile, width), BF)],
        compiler_params=pltpu.CompilerParams(vmem_limit_bytes=16 * MIB),
        cost_estimate=cost(3),
    )(own, *pieces)


def attn_bwd_kernel(
    own_ref,
    *refs,
):
    items, refs = refs[:8], refs[8:]
    (
    cot_blk,
    res_ref,
    ctx_ref,
    qkv_ref,
    tok_ref,
    code_ref,
    w_ref,
    gain_ref,
    wr_ref,
    *gtok_refs,
    keep_ref,
    give_ref,
    acc,
    rows_acc,
    sums,
    n2_ref,
    gtok_ref,
    ) = refs
    cot_ref = cot_blk.at[0]
    own = own_ref[0]
    img = pl.program_id(0)
    seq_len, width = n2_ref.shape

    @pl.when(img == 0)
    def _():
        acc[...] = jnp.zeros_like(acc)
        rows_acc[...] = jnp.zeros_like(rows_acc)

    half = pl.num_programs(0) // 2
    for side in range(2):

        @pl.when((img >= side * half) & (img < (side + 1) * half))
        def _():
            d0, d1, d2, n2 = (items[2 * t + side] for t in range(4))
            sums[...] = d0[0].astype(F32) + d1[0].astype(F32) + d2[0].astype(F32)
            n2_ref[...] = n2[0]

    code = code_ref[:, 0].reshape(seq_len, 128)[:, 0:1].astype(F32)
    keep = (code.astype(jnp.int32) & 1) > 0
    total = sums[...]
    n2 = n2_ref[...]
    probs, chosen = router(own, n2, wr_ref[...], cot_ref[seq_len : seq_len + 1, :seq_len])
    gate_grad = chosen * total[width : width + 8]
    logit_grad = probs * (gate_grad - jnp.sum(probs * gate_grad, axis=0, keepdims=True))
    high = logit_grad.astype(BF)
    low = (logit_grad - high.astype(F32)).astype(BF)
    rows_acc[16:24] += dot(high, n2) + dot(low, n2)
    wr = wr_ref[...].astype(BF)
    dn2 = (total[:width] + dot(wr, high, TN) + dot(wr, low, TN)).T
    hat2, inv2 = norm(res_ref[0])
    rows_acc[1:2] += jnp.sum(dn2 * hat2, axis=0, keepdims=True)
    res_grad = cot_ref[:seq_len].astype(F32) + norm_back(dn2 * gain_ref[1:2], hat2, inv2)
    pg = jnp.where(keep, res_grad, 0.0).astype(BF)
    acc[:, 3 * width :] += dot(ctx_ref[0], pg, TN)
    dctx = dot(pg, w_ref[:, 3 * width : 4 * width], NT).astype(BF)
    dqs, dks, dvs = [], [], []
    for h in range(HEADS):
        q = qkv_ref[0, :, h * HEAD : (h + 1) * HEAD]
        k = qkv_ref[0, :, width + h * HEAD : width + (h + 1) * HEAD]
        v = qkv_ref[0, :, 2 * width + h * HEAD : 2 * width + (h + 1) * HEAD]
        do = dctx[:, h * HEAD : (h + 1) * HEAD]
        s = jnp.where(keep, dot(k, q, NT) * 0.125, -1e30)
        e = jnp.exp(s - jnp.max(s, axis=0, keepdims=True))
        p = e * (1.0 / jnp.sum(e, axis=0, keepdims=True))
        dvs.append(dot(p.astype(BF), do))
        wg = dot(v, do, NT)
        sg = (p * (wg - jnp.sum(p * wg, axis=0, keepdims=True))).astype(BF)
        dqs.append(dot(sg, k, TN) * 0.125)
        dks.append(dot(sg, q) * 0.125)
    dqkv = jnp.concatenate(dqs + dks + dvs, axis=1).astype(BF)
    hat, inv = norm(tok_ref[:, 0].reshape(seq_len, width).astype(F32))
    n1 = (hat * gain_ref[0:1]).astype(BF)
    acc[:, : 3 * width] += dot(n1, dqkv, TN)
    dn1 = dot(dqkv, w_ref[:, : 3 * width], NT)
    rows_acc[0:1] += jnp.sum(dn1 * hat, axis=0, keepdims=True)
    gtok = res_grad + norm_back(dn1 * gain_ref[0:1], hat, inv)
    gtok = jnp.where(keep, gtok, 0.0).astype(BF)
    gtok_ref[...] = gtok.reshape(gtok_ref.shape)
    for r, ref in enumerate(gtok_refs):
        ref[0] = gtok_ref[own ^ r]

    @pl.when(img == pl.num_programs(0) - 1)
    def _():
        for r in range(4):
            rows_acc[pl.ds(8 + (own ^ r), 1)] = rows_acc[16 + r : 17 + r]
        tail = rows_acc[...].T.astype(BF)
        mid = keep_ref.shape[1]
        for core, left, right in ((0, keep_ref, give_ref), (1, give_ref, keep_ref)):

            @pl.when((own & 1) == core)
            def _():
                left[...] = acc[:, :mid].astype(BF)
                right[:, : 4 * width - mid] = acc[:, mid:].astype(BF)
                right[:, 4 * width - mid :] = tail


def attn_bwd(own, d0, d1, d2, n2, cot, res, ctx, qkv, tok, code, w, gains, wr):
    images, seq_len, width = res.shape
    parts, _, seg, _ = tok.shape
    half = images // 2
    item = lambda a: pl.BlockSpec((1,) + a.shape[1:], lambda i, *_: (i, 0, 0))
    whole = lambda a: pl.BlockSpec(a.shape, lambda i, *_: (0, 0))
    cols = 4 * width + SMALL

    def side(a, k):
        return pl.BlockSpec(
            (1,) + a.shape[1:], lambda i, *_: (jnp.clip(i - k * half, 0, half - 1), 0, 0)
        )

    halves = [*d0, *d1, *d2, *n2]
    return pl.pallas_call(
        attn_bwd_kernel,
        grid_spec=pltpu.PrefetchScalarGridSpec(
            num_scalar_prefetch=1,
            grid=(images,),
            in_specs=[side(a, k % 2) for k, a in enumerate(halves)]
            + [item(a) for a in (cot, res, ctx, qkv)]
            + [
                pl.BlockSpec((parts, 1, seg, width), lambda i, *_: (0, i, 0, 0)),
                pl.BlockSpec((parts, 1, seg, 128), lambda i, *_: (0, i, 0, 0)),
            ]
            + [whole(a) for a in (w, gains, wr)],
            out_specs=[
                *[pl.BlockSpec((1, seg, width), lambda i, *_: (i, 0, 0))] * 4,
                pl.BlockSpec((width, cols // 2), lambda i, *_: (0, 0)),
                pl.BlockSpec((width, cols // 2), lambda i, *_: (0, 0)),
            ],
            scratch_shapes=[
                pltpu.VMEM((width, 4 * width), F32),
                pltpu.VMEM((SMALL, width), F32),
                pltpu.VMEM(d0[0].shape[1:], F32),
                pltpu.VMEM((seq_len, width), BF),
                pltpu.VMEM((parts, seg, width), BF),
            ],
        ),
        out_shape=[
            *[jax.ShapeDtypeStruct((images, seg, width), BF)] * 4,
            jax.ShapeDtypeStruct((width, cols // 2), BF),
            jax.ShapeDtypeStruct((width, cols // 2), BF),
        ],
        compiler_params=pltpu.CompilerParams(vmem_limit_bytes=30 * MIB),
        cost_estimate=cost(17),
    )(own, *halves, cot, res, ctx, qkv, tok, code, w, gains, wr)


def result_kernel(own_ref, *refs):
    outs, res_ref, code_ref, out_refs, sums, parts = refs[:5], refs[5], refs[6], refs[7:11], *refs[11:]
    img = pl.program_id(0)
    half = pl.num_programs(0) // 2
    seq_len, width = res_ref.shape[1:]
    for side in range(2):

        @pl.when((img >= side * half) & (img < (side + 1) * half))
        def _():
            one, two = outs[1 + side], outs[3 + side]
            sums[...] = outs[0][0].astype(F32) + one[0].astype(F32) + two[0].astype(F32)

    code = code_ref[:, 0].reshape(seq_len, 128)[:, 0:1].astype(F32)
    keep = (code.astype(jnp.int32) & 1) > 0
    out = (res_ref[0] + jnp.where(keep, sums[...].T, 0.0)).astype(BF)
    parts[...] = out.reshape(parts.shape)
    for r, ref in enumerate(out_refs):
        ref[0] = parts[own_ref[0] ^ r]


def result(own, outs, o1, o2, res, code):
    images, seq_len, width = res.shape
    parts, _, seg, _ = code.shape
    half = images // 2

    def side(k):
        return pl.BlockSpec(
            (1, width, seq_len), lambda i: (jnp.clip(i - k * half, 0, half - 1), 0, 0)
        )

    return pl.pallas_call(
        result_kernel,
        grid=(images,),
        in_specs=[
            pl.BlockSpec(memory_space=pltpu.SMEM),
            pl.BlockSpec((1, width, seq_len), lambda i: (i, 0, 0)),
            side(0),
            side(1),
            side(0),
            side(1),
            pl.BlockSpec((1, seq_len, width), lambda i: (i, 0, 0)),
            pl.BlockSpec((parts, 1, seg, 128), lambda i: (0, i, 0, 0)),
        ],
        out_specs=[pl.BlockSpec((1, seg, width), lambda i: (i, 0, 0))] * 4,
        out_shape=[jax.ShapeDtypeStruct((images, seg, width), BF)] * 4,
        scratch_shapes=[
            pltpu.VMEM((width, seq_len), F32),
            pltpu.VMEM((parts, seg, width), BF),
        ],
        compiler_params=pltpu.CompilerParams(vmem_limit_bytes=12 * MIB),
        cost_estimate=cost(2),
    )(own, outs, *o1, *o2, res, code)


def gather_images_kernel(own_ref, p0, p1, p2, p3, out_ref):
    for r, piece in enumerate((p0, p1, p2, p3)):
        out_ref[own_ref[0] ^ r] = piece[...].astype(out_ref.dtype)


def gather_images(own, pieces, dtype):
    whole = pl.BlockSpec(memory_space=pltpu.VMEM)
    shape = pieces[0].shape
    out = pl.pallas_call(
        gather_images_kernel,
        in_specs=[pl.BlockSpec(memory_space=pltpu.SMEM)] + [whole] * 4,
        out_specs=whole,
        out_shape=jax.ShapeDtypeStruct((4,) + shape, dtype),
        compiler_params=pltpu.CompilerParams(vmem_limit_bytes=8 * MIB),
        cost_estimate=cost(1),
    )(own, *pieces)
    return out.reshape((4 * shape[0],) + shape[1:])


def finish_kernel(own_ref, mine_ref, other_ref, qkv_ref, proj_ref, small_ref):
    mid = mine_ref.shape[1]
    rest = qkv_ref.shape[1] - mid
    width = proj_ref.shape[1]
    for core, left, right in ((0, mine_ref, other_ref), (1, other_ref, mine_ref)):

        @pl.when((own_ref[0] & 1) == core)
        def _():
            qkv_ref[:, :mid] = left[...].astype(F32)
            qkv_ref[:, mid:] = right[:, :rest].astype(F32)
            proj_ref[...] = right[:, rest : rest + width].astype(F32)
            small_ref[...] = right[:, rest + width : rest + width + 128].astype(F32)


def finish(own, mine, other, width):
    rows = mine.shape[0]
    whole = pl.BlockSpec(memory_space=pltpu.VMEM)
    shape = lambda w: jax.ShapeDtypeStruct((rows, w), F32)
    return pl.pallas_call(
        finish_kernel,
        in_specs=[pl.BlockSpec(memory_space=pltpu.SMEM), whole, whole],
        out_specs=[whole] * 3,
        out_shape=[shape(3 * width), shape(width), shape(128)],
        compiler_params=pltpu.CompilerParams(vmem_limit_bytes=8 * MIB),
        cost_estimate=cost(1),
    )(own, mine, other)


def ring_gather(x, m, fw, bw, cut):
    ahead, behind = [], []
    a = b = x
    for _ in range(m // 2 - 1):
        a, b = send(a, "fsdp", fw), send(b, "fsdp", bw)
        ahead.append(a)
        behind.append(b)
    return ahead, behind, send(cut(a)[0], "fsdp", fw), send(cut(b)[1], "fsdp", bw)


def halves_gather(parts, m, fw, bw, last=lambda a: a):
    ahead, behind = [], []
    f, b = list(parts), list(parts)
    for _ in range(m // 2 - 1):
        first, second = send(f[0], "fsdp", fw), send(b[1], "fsdp", bw)
        f, b = [first, send(f[1], "fsdp", fw)], [send(b[0], "fsdp", bw), second]
        ahead.append(f)
        behind.append(b)
    return ahead, behind, send(last(f[0]), "fsdp", fw), send(last(b[1]), "fsdp", bw)


def halves_scatter(ahead, behind, far, fw, bw, wait=lambda a: a, seen=None):
    out = []
    for terms, pairs, whole in ((ahead, fw, 0), (behind, bw, 1)):
        got = [None, None]
        for half in (whole, 1 - whole):
            acc = far[half] if half == whole else None
            for term in reversed(terms):
                acc = term[half] if acc is None else add_low(term[half], wait(send(acc, "fsdp", pairs)))
                if seen is not None and half == whole:
                    seen.append(acc)
            got[half] = send(acc, "fsdp", pairs)
        out.append(got)
    return out


def ring_scatter(ahead, behind, top, bottom, fw, bw, put):
    a, b = send(top, "fsdp", fw), send(bottom, "fsdp", bw)
    for step, (to_fw, to_bw) in enumerate(zip(reversed(ahead), reversed(behind))):
        if step == 0:
            a, b = put(to_fw, a, 0), put(to_bw, b, 1)
        else:
            a, b = add_low(jnp.concatenate(to_fw), a), add_low(jnp.concatenate(to_bw), b)
        a, b = send(a, "fsdp", fw), send(b, "fsdp", bw)
    return a, b


def after(x, *done):
    return lax.optimization_barrier((x,) + done)[0]


def per_device(
    tokens, pad_mask, routes, ln1_gain, w_qkv, w_proj, ln2_gain, w_router, exp_in, exp_out, cotangent
):
    n = lax.axis_size("fsdp")
    per_device_images, seg, width = tokens.shape
    seq_idx = lax.axis_index("seq")
    own = seq_idx.astype(jnp.int32).reshape(1)
    idx = lax.axis_index("fsdp")
    m = n // 2
    fw8, bw8 = ring_pairs([ring_order(n)])
    low_ring = ring_order(m)
    fw4, bw4 = ring_pairs([low_ring, [m + i for i in low_ring]])
    pair = [(i, (i + m) % n) for i in range(n)]
    by_core = [(i, i ^ 1) for i in range(4)]
    by_half = [(i, i ^ 2) for i in range(4)]

    rows = w_qkv.shape[0]
    small = jnp.concatenate([ln1_gain[:, None], ln2_gain[:, None]], axis=1)
    small = jnp.pad(small, ((0, 0), (0, SMALL - 2))) + jnp.pad(
        w_router, ((0, 0), (8, SMALL - 12))
    )
    block = block_of(own, w_qkv, w_proj, small)
    mid = block.shape[1]

    fr = exp_in.shape[0]
    pick = lambda a: lax.dynamic_index_in_dim(a, seq_idx, 1, False)
    mine = jnp.stack([pick(exp_in), pick(exp_out)]).astype(BF)
    part = lambda k: mine[:, k * fr // 2 : (k + 1) * fr // 2]

    keep = pad_mask.astype(BF)[..., None]
    code = pad_mask + 2 * routes[..., 0] + 8 * routes[..., 1]
    code = jnp.pad(code.astype(BF)[..., None], ((0, 0), (0, 0), (0, 127)))
    fused = jnp.concatenate([tokens * keep, cotangent * keep, code], axis=2)
    images = per_device_images // 4
    half_img = images // 2
    fused = fused.reshape(4, images, seg, 2 * width + 128)
    by_seq = [[(i, i ^ r) for i in range(4)] for r in range(4)]
    pieces = [lax.dynamic_index_in_dim(fused, seq_idx ^ r, 0, False) for r in range(4)]
    swap = lambda parts: [parts[0]] + [send(parts[r], "seq", by_seq[r]) for r in (3, 2, 1)][::-1]
    tok, codes, cot = unpack(own, swap(pieces), width)

    base = jnp.where(idx < m, 0, m)
    spot = idx - base
    place = jnp.where(spot % 2 == 0, spot // 2, m - 1 - spot // 2)

    def member(p):
        p = p % m
        return jnp.where(p < m // 2, 2 * p, 2 * (m - 1 - p) + 1)

    chunk = jnp.stack([block, send(block, "fsdp", pair)])
    ahead, behind, top, bottom = ring_gather(
        chunk, m, fw4, bw4, lambda a: after((a[:1], a[1:]), tok)
    )
    q0 = send(after(mine, chunk), "fsdp", pair)

    pieces, offs = [chunk], [idx, (idx + m) % n]
    for d in range(1, m // 2):
        for got, i in ((ahead, member(place - d + m)), (behind, member(place + d))):
            pieces.append(got[d - 1])
            offs += [base + i, m - base + i]
    far_member = member(place + m // 2)
    pieces += [top, bottom]
    offs += [base + far_member, m - base + far_member]
    offs = jnp.stack(offs).astype(jnp.int32) * rows
    w_mine = gather_rows(pieces, offs, (n * rows, mid))
    w_other = send(w_mine, "seq", by_core)

    late_in, late_out = after((exp_in, exp_out), q0)
    win = late_in.transpose(1, 0, 2).astype(BF)
    wout = late_out.transpose(1, 0, 2).astype(BF)
    *n2, res, qkv, ctx, w, gains, wr = attn_fwd(own, tok, codes, w_mine, w_other)
    g_ahead, g_behind, g_top, g_bottom = ring_gather(
        after(cot, top, bottom),
        m,
        fw4,
        bw4,
        lambda a: after((a[:half_img], a[half_img:]), *n2),
    )
    q2 = send(q0, "seq", by_half)
    quarters = [q0, send(q0, "seq", by_core), q2, send(q2, "seq", by_core)]

    win, wout, wint, woutt = weights(own, win, wout, quarters)
    units = images * m
    bufs, at = None, 0

    def experts(xs, gs):
        nonlocal at, bufs
        *dd, b0, b1, b2, b3 = moe_call(
            xs, gs, own, wr, win, wout, wint, at, units, bufs
        )
        bufs = [b0, b1, b2, b3]
        at += images
        return dd

    d_own = experts(n2, [(cot, 0), (cot, half_img)])
    x_ahead, x_behind, x_top, x_bottom = halves_gather(
        n2, m, fw4, bw4, lambda a: after(a, *d_own)
    )
    dx_ahead, dx_behind, where = [], [], []
    for d in range(m // 2 - 1):
        (xa, xb), (ga, gb) = (x_ahead[d], x_behind[d]), (g_ahead[d], g_behind[d])
        where.append(at)
        back0, on1 = experts([xa[0], xb[1]], [(ga, 0), (gb, half_img)])
        back1, on0 = experts([xa[1], xb[0]], [(ga, half_img), (gb, 0)])
        dx_ahead.append([on0, on1])
        dx_behind.append([back0, back1])
    far_at = at
    far = experts([x_top, x_bottom], [(g_top, 0), (g_bottom, 0)])
    ga, hg, xb, gb = bufs

    grad3 = moe_grad(ga, hg, xb, gb, 3)
    grad2 = moe_grad(after(ga, grad3), hg, xb, gb, 2)
    grad1 = moe_grad(after(ga, grad2), hg, xb, gb, 1)
    seen = []
    d1, d2 = halves_scatter(
        dx_ahead, dx_behind, far, fw4, bw4, lambda a: after(a, grad1), seen
    )
    kept2 = add_low(grad2, send(grad3, "seq", by_core))
    grad0 = moe_grad(after(ga, kept2, *seen), hg, xb, gb, 0)
    kept0 = add_low(grad0, send(grad1, "seq", by_core))
    outs = moe_out(woutt, after(ga, grad0))
    first_half = send(kept2[1], "seq", by_half)
    d_own = [after(d_own[0], grad0), d_own[1]]

    *gtok, dw_keep, dw_give = attn_bwd(
        own, d_own, d1, d2, n2, cot, res, ctx, qkv, tok, codes, w, gains, wr
    )

    outs = after(outs, *d1, *d2)
    out_at = lambda k: outs[k : k + half_img]
    o_ahead = [[out_at(k + 3 * half_img), out_at(k + half_img)] for k in where]
    o_behind = [[out_at(k), out_at(k + 2 * half_img)] for k in where]
    firsts = []

    def hold(a):
        firsts.append(a)
        return after(a, dw_keep)

    o1, o2 = halves_scatter(
        o_ahead, o_behind, (out_at(far_at), out_at(far_at + half_img)), fw4, bw4, hold
    )
    kept_pair = add_low(kept0[1], after(first_half, dw_keep))
    from_pair = send(kept_pair, "fsdp", pair)

    dw_give = after(dw_give, first_half, *firsts[: 2 if m == 4 else 0])
    dw = add_low(dw_keep, send(dw_give, "seq", by_core))

    def term(i):
        cut = lambda k: lax.dynamic_slice_in_dim(dw, k * rows, rows, 0)[None]
        return [cut(base + i), cut(m - base + i)]

    def put_part(t, part, side):
        t = list(t)
        t[side] = add_low(t[side], part)
        return jnp.concatenate(t)

    last = term(far_member)
    s1, s2 = ring_scatter(
        [term(member(place + d)) for d in range(1, m // 2)],
        [term(member(place - d + m)) for d in range(1, m // 2)],
        last[0],
        last[1],
        fw4,
        bw4,
        put_part,
    )
    low = lambda a: a.astype(F32)
    mine_t, pair_t = term(spot)
    for_pair = (low(pair_t) + low(s1[1:]) + low(s2[1:])).astype(BF)
    dense = (low(mine_t) + low(s1[:1]) + low(s2[:1]) + low(send(for_pair, "fsdp", pair)))[0].astype(BF)
    dense = add_low(dense, send(dense, "seq", by_half))
    g_qkv, g_proj, g_small = finish(own, dense, send(dense, "seq", by_core), width)

    grad_tokens = gather_images(own, swap([after(g, s1) for g in gtok]), F32)
    block_out = gather_images(own, swap(result(own, outs, o1, o2, res, codes)), BF)

    from_half = after(send(kept2[0], "seq", by_half), dw_keep)
    quarter = add_low(add_low(kept0[0], from_half), from_pair)
    from_half = send(quarter, "seq", by_half)
    grad_in, grad_out = pack(
        own,
        [quarter, send(quarter, "seq", by_core), from_half, send(from_half, "seq", by_core)],
    )

    return (
        block_out,
        grad_tokens,
        g_small[:, 0],
        g_qkv,
        g_proj,
        g_small[:, 1],
        g_small[:, 8:12],
        grad_in,
        grad_out,
    )


def solution(mesh):
    row = P("fsdp", None)
    cube = P("fsdp", None, None)
    split = P("fsdp", "seq", None)
    return jax.shard_map(
        per_device,
        mesh=mesh,
        in_specs=(
            split,
            P("fsdp", "seq"),
            split,
            P("fsdp"),
            row,
            row,
            P("fsdp"),
            row,
            cube,
            cube,
            split,
        ),
        out_specs=(split, split, P("fsdp"), row, row, P("fsdp"), row, cube, cube),
        check_vma=False,
    )
```

profile of v0, /device:TPU:0, one launch (start us, length us, event | category | flops | bytes accessed | tf_op | source)
XLA Modules:
  0.0 222.4 jit_solution(1176928361996359176)
XLA Ops:
  4.2 4.1 %collective-permute-start = (bf16[64,1152]{1,0:T(8,128)(2,1)S(1)}, bf16[64,1152]{1,0:T(8,128)(2,1)S(1)}, u32[]{:S(2)}, u32[]{:S(2)}) collective-permute-start(bf16[64,1152]{1,0:T(8,128)(2,1)S(1)} %shard_map.178), channel_id=1, source_target_pairs={{0,4},{1,5},{2,6},{3,7},{4,0},{5,1},{6,2},{7,3},{8,12},{9,13},{10,... | collective-permute-start | bytes 442376 | tf_op jit(solution)/shard_map/ppermute | solution.py:46
  10.1 1.3 broadcast_multiply_fusion.1
  12.4 1.5 collective-permute-start.6
  15.4 1.6 collective-permute-start.9
  17.4 3.2 %constant_dynamic-slice_fusion = (bf16[256,1,512]{2,1,0:T(2,128)(2,1)S(1)}, bf16[256,1,512]{2,1,0:T(2,128)(2,1)S(1)}) fusion(f32[256,4,512]{2,1,0:T(4,128)} %param.20, s32[]{:T(128)S(6)} %select_n.90, f32[256,4,512]{2,1,0:T(4,128)} %param.19), kind=kLoop, calls=%fused_computation.60 | loop fusion | bytes 1048580 | tf_op jit(solution)/shard_map/jit(dynamic_index_in_dim)/dynamic_slice | solution.py:842
  20.9 2.2 collective-permute-start.1
  23.1 4.6 %collective-permute-done.7.p3 = bf16[2,64,1152]{2,1,0:T(8,128)(2,1)S(1)} collective-permute-done((bf16[2,64,1152]{2,1,0:T(8,128)(2,1)S(1)}, bf16[2,64,1152]{2,1,0:T(8,128)(2,1)S(1)}, u32[]{:S(2)}, u32[]{:S(2)}) %collective-permute-start.7) | collective-permute-done | bytes 294944 | tf_op jit(solution)/shard_map/ppermute | solution.py:46
  28.1 1.6 collective-permute-start.11
  30.2 4.2 %collective-permute-done.11.a_5_ = bf16[1,64,1152]{2,1,0:T(8,128)(2,1)S(1)} collective-permute-done((bf16[1,64,1152]{2,1,0:T(8,128)(2,1)S(1)}, bf16[1,64,1152]{2,1,0:T(8,128)(2,1)S(1)}, u32[]{:S(2)}, u32[]{:S(2)}) %collective-permute-start.11) | collective-permute-done | bytes 147488 | tf_op jit(solution)/shard_map/ppermute | solution.py:46
  34.4 3.0 %collective-permute-done.10.a_4_ = bf16[1,64,1152]{2,1,0:T(8,128)(2,1)S(1)} collective-permute-done((bf16[1,64,1152]{2,1,0:T(8,128)(2,1)S(1)}, bf16[1,64,1152]{2,1,0:T(8,128)(2,1)S(1)}, u32[]{:S(2)}, u32[]{:S(2)}) %collective-permute-start.10) | collective-permute-done | bytes 147488 | tf_op jit(solution)/shard_map/ppermute | solution.py:46
  37.4 2.2 shard_map.181.mine_ref
  39.6 6.5 %collective-permute-done.1.refs_2_ = bf16[2,256,512]{2,1,0:T(8,128)(2,1)S(1)} collective-permute-done((bf16[2,256,512]{2,1,0:T(8,128)(2,1)S(1)}, bf16[2,256,512]{2,1,0:T(8,128)(2,1)S(1)}, u32[]{:S(2)}, u32[]{:S(2)}) %collective-permute-start.1) | collective-permute-done | bytes 524320 | tf_op jit(solution)/shard_map/ppermute | solution.py:46
  46.1 1.5 collective-permute-start.3
  49.7 8.6 %collective-permute-done.3.refs_4_ = bf16[2,256,512]{2,1,0:T(8,128)(2,1)S(1)} collective-permute-done((bf16[2,256,512]{2,1,0:T(8,128)(2,1)S(1)}, bf16[2,256,512]{2,1,0:T(8,128)(2,1)S(1)}, u32[]{:S(2)}, u32[]{:S(2)}) %collective-permute-start.3) | collective-permute-done | bytes 524320 | tf_op jit(solution)/shard_map/ppermute | solution.py:46
  58.3 7.0 %shard_map.182 = (bf16[1,256,512]{2,1,0:T(8,128)(2,1)S(1)}, bf16[1,256,512]{2,1,0:T(8,128)(2,1)S(1)}, f32[2,256,512]{2,1,0:T(8,128)S(1)}, bf16[2,256,1536]{2,1,0...) custom-call(s32[1]{0:T(128)} %bitcast.own_ref.a_0_, ...), custom_call_target="tpu_custom_call" | custom-call | flops 920001 | bytes 81 | tf_op jit(solution)/shard_map/pallas_call | solution.py:225
  65.3 1.5 collective-permute-start.15
  67.9 1.9 collective-permute-start.21
  70.1 1.9 collective-permute-start.18
  73.2 1.3 shard_map.179
  74.5 4.5 %shard_map.183 = (bf16[1,528,256]{2,1,0:T(8,128)(2,1)S(1)}, bf16[1,528,256]{2,1,0:T(8,128)(2,1)S(1)}, bf16[8,2048,256]{2,1,0:T(8,128)(2,1)S(1)}, bf16[8,2048,256...) custom-call(s32[1]{0:T(128)} %bitcast.own_ref.a_0_, ...), custom_call_target="tpu_custom_call" | custom-call | flops 598001 | bytes 53 | tf_op jit(solution)/shard_map/pallas_call | solution.py:383
  79.2 1.4 collective-permute-start.16
  80.6 1.4 collective-permute-done.21.a_5_
  82.6 4.5 %shard_map.184 = (bf16[1,528,256]{2,1,0:T(8,128)(2,1)S(1)}, bf16[1,528,256]{2,1,0:T(8,128)(2,1)S(1)}, bf16[8,2048,256]{2,1,0:T(8,128)(2,1)S(1)}, bf16[8,2048,256...) custom-call(s32[1]{0:T(128)} %bitcast.own_ref.a_0_, ...), custom_call_target="tpu_custom_call", output_to_operand_aliasing={{2}: (9, {}), {3}: (10, {}), {4}: (11, {}), {5}: (12, {})} | custom-call | flops 598001 | bytes 53 | tf_op jit(solution)/shard_map/pallas_call | solution.py:383
  88.3 4.5 %shard_map.185 = (bf16[1,528,256]{2,1,0:T(8,128)(2,1)S(1)}, bf16[1,528,256]{2,1,0:T(8,128)(2,1)S(1)}, bf16[8,2048,256]{2,1,0:T(8,128)(2,1)S(1)}, bf16[8,2048,256...) custom-call(s32[1]{0:T(128)} %bitcast.own_ref.a_0_, ...), custom_call_target="tpu_custom_call", output_to_operand_aliasing={{2}: (9, {}), {3}: (10, {}), {4}: (11, {}), {5}: (12, {})} | custom-call | flops 598001 | bytes 53 | tf_op jit(solution)/shard_map/pallas_call | solution.py:383
  93.2 4.4 %shard_map.186 = (bf16[1,528,256]{2,1,0:T(8,128)(2,1)S(1)}, bf16[1,528,256]{2,1,0:T(8,128)(2,1)S(1)}, bf16[8,2048,256]{2,1,0:T(8,128)(2,1)S(1)}, bf16[8,2048,256...) custom-call(s32[1]{0:T(128)} %bitcast.own_ref.a_0_, ...), custom_call_target="tpu_custom_call", output_to_operand_aliasing={{2}: (9, {}), {3}: (10, {}), {4}: (11, {}), {5}: (12, {})} | custom-call | flops 598001 | bytes 53 | tf_op jit(solution)/shard_map/pallas_call | solution.py:383
  97.6 2.8 %shard_map.187 = bf16[2,2,256,512]{3,2,1,0:T(8,128)(2,1)S(1)} custom-call(bf16[8,2048,256]{2,1,0:T(8,128)(2,1)S(1)} %get-tuple-element.137.a_0_.ga_ref, bf16[8,2048,256]{2,1,0:T(8,128)(2,1)S(1)} %get-tuple-element.125.a_1_, bf16[8,256,512]{2,1,0:T(8,128)(2,1)S(1)} %get-tuple-element.126.a_2_, bf16[8,272,512]{2,1,0:T(8,128)(2,1)S(1)} %get-tuple-element.127.a_3_), custom_call_target="tpu_custom_call" | custom-call | flops 432401 | bytes 38 | tf_op jit(solution)/shard_map/pallas_call | solution.py:469
  100.6 1.8 collective-permute-start.25
  104.7 2.8 %shard_map.188 = bf16[2,2,256,512]{3,2,1,0:T(8,128)(2,1)S(1)} custom-call(bf16[8,2048,256]{2,1,0:T(8,128)(2,1)S(1)} %get-tuple-element.137.a_0_.ga_ref, bf16[8,2048,256]{2,1,0:T(8,128)(2,1)S(1)} %get-tuple-element.125.a_1_, bf16[8,256,512]{2,1,0:T(8,128)(2,1)S(1)} %get-tuple-element.126.a_2_, bf16[8,272,512]{2,1,0:T(8,128)(2,1)S(1)} %get-tuple-element.127.a_3_), custom_call_target="tpu_custom_call" | custom-call | flops 432401 | bytes 38 | tf_op jit(solution)/shard_map/pallas_call | solution.py:469
  107.5 3.6 %shard_map.189 = bf16[2,2,256,512]{3,2,1,0:T(8,128)(2,1)} custom-call(bf16[8,2048,256]{2,1,0:T(8,128)(2,1)S(1)} %get-tuple-element.137.a_0_.ga_ref, bf16[8,2048,256]{2,1,0:T(8,128)(2,1)S(1)} %get-tuple-element.125.a_1_, bf16[8,256,512]{2,1,0:T(8,128)(2,1)S(1)} %get-tuple-element.126.a_2_, bf16[8,272,512]{2,1,0:T(8,128)(2,1)S(1)} %get-tuple-element.127.a_3_), custom_call_target="tpu_custom_call" | custom-call | flops 432401 | bytes 38 | tf_op jit(solution)/shard_map/pallas_call | solution.py:469
  115.1 1.5 collective-permute-start.39
  116.6 2.8 %shard_map.190 = bf16[2,2,256,512]{3,2,1,0:T(8,128)(2,1)S(1)} custom-call(bf16[8,2048,256]{2,1,0:T(8,128)(2,1)S(1)} %get-tuple-element.137.a_0_.ga_ref, bf16[8,2048,256]{2,1,0:T(8,128)(2,1)S(1)} %get-tuple-element.125.a_1_, bf16[8,256,512]{2,1,0:T(8,128)(2,1)S(1)} %get-tuple-element.126.a_2_, bf16[8,272,512]{2,1,0:T(8,128)(2,1)S(1)} %get-tuple-element.127.a_3_), custom_call_target="tpu_custom_call" | custom-call | flops 432401 | bytes 38 | tf_op jit(solution)/shard_map/pallas_call | solution.py:469
  120.4 5.8 %shard_map.191.refs_0_ = bf16[8,512,256]{2,1,0:T(8,128)(2,1)S(1)} custom-call(bf16[512,2048]{1,0:T(8,128)(2,1)S(1)} %get-tuple-element.93.woutt_ref, bf16[8,2048,256]{2,1,0:T(8,128)(2,1)S(1)} %get-tuple-element.137.a_0_.ga_ref), custom_call_target="tpu_custom_call" | custom-call | flops 644001 | bytes 57 | tf_op jit(solution)/shard_map/pallas_call | solution.py:420
  127.7 1.5 collective-permute-start.34
  129.2 14.2 %shard_map.192 = (bf16[2,64,512]{2,1,0:T(8,128)(2,1)S(1)}, bf16[2,64,512]{2,1,0:T(8,128)(2,1)S(1)}, bf16[2,64,512]{2,1,0:T(8,128)(2,1)S(1)}, bf16[2,64,512]{2,1,...) custom-call(s32[1]{0:T(128)} %bitcast.own_ref.a_0_, ...), custom_call_target="tpu_custom_call" | custom-call | flops 1955001 | bytes 171 | tf_op jit(solution)/shard_map/pallas_call | solution.py:630
  148.1 1.6 collective-permute-done.40
  149.7 2.0 add_convert_fusion
  152.4 1.5 collective-permute-start.46
  153.9 1.5 add_convert_fusion.1
  155.4 3.5 %collective-permute-done.41 = bf16[1,64,1152]{2,1,0:T(8,128)(2,1)S(1)} collective-permute-done((bf16[1,64,1152]{2,1,0:T(8,128)(2,1)S(1)}, bf16[1,64,1152]{2,1,0:T(8,128)(2,1)S(1)}, u32[]{:S(2)}, u32[]{:S(2)}) %collective-permute-start.41) | collective-permute-done | bytes 147488 | tf_op jit(solution)/shard_map/ppermute | solution.py:46
  162.4 3.4 %collective-permute-start.53 = (bf16[2,256,512]{2,1,0:T(8,128)(2,1)S(1)}, bf16[2,256,512]{2,1,0:T(8,128)(2,1)S(1)}, u32[]{:S(2)}, u32[]{:S(2)}) collective-permute-start(bf16[2,256,512]{2,1,0:T(8,128)(2,1)S(1)} %fusion.4), channel_id=1, source_target_pairs={{0,4},{1,5},{2,6},{3,7},{4,0},{5,1},{6,2},{7,3},{8,12},{9,13},{10,... | collective-permute-start | bytes 1572872 | tf_op jit(solution)/shard_map/ppermute | solution.py:46
  167.2 6.3 %collective-permute-done.47 = bf16[2,64,1152]{2,1,0:T(8,128)(2,1)S(1)} collective-permute-done((bf16[2,64,1152]{2,1,0:T(8,128)(2,1)S(1)}, bf16[2,64,1152]{2,1,0:T(8,128)(2,1)S(1)}, u32[]{:S(2)}, u32[]{:S(2)}) %collective-permute-start.47) | collective-permute-done | bytes 294944 | tf_op jit(solution)/shard_map/ppermute | solution.py:46
  173.5 2.2 %collective-permute-start.35 = (bf16[1,512,256]{2,1,0:T(8,128)(2,1)S(1)}, bf16[1,512,256]{2,1,0:T(8,128)(2,1)S(1)}, u32[]{:S(2)}, u32[]{:S(2)}) collective-permute-start(bf16[1,512,256]{2,1,0:T(8,128)(2,1)S(1)} %get-tuple-element.200), channel_id=1, source_target_pairs={{2,0},{3,2},{1,3},{0,1},{6,4},{7,6},{5,7},{4,5},{10,8},{11,10},{9,... | collective-permute-start | bytes 786440 | tf_op jit(solution)/shard_map/ppermute | solution.py:46
  175.8 12.0 %collective-permute-done.53 = bf16[2,256,512]{2,1,0:T(8,128)(2,1)S(1)} collective-permute-done((bf16[2,256,512]{2,1,0:T(8,128)(2,1)S(1)}, bf16[2,256,512]{2,1,0:T(8,128)(2,1)S(1)}, u32[]{:S(2)}, u32[]{:S(2)}) %collective-permute-start.53) | collective-permute-done | bytes 524320 | tf_op jit(solution)/shard_map/ppermute | solution.py:46
  188.0 8.0 %collective-permute-done.48 = bf16[1,64,1152]{2,1,0:T(8,128)(2,1)S(1)} collective-permute-done((bf16[1,64,1152]{2,1,0:T(8,128)(2,1)S(1)}, bf16[1,64,1152]{2,1,0:T(8,128)(2,1)S(1)}, u32[]{:S(2)}, u32[]{:S(2)}) %collective-permute-start.48) | collective-permute-done | bytes 147488 | tf_op jit(solution)/shard_map/ppermute | solution.py:46
  200.8 6.8 %collective-permute-done.55.refs_2_ = bf16[2,256,512]{2,1,0:T(8,128)(2,1)S(1)} collective-permute-done((bf16[2,256,512]{2,1,0:T(8,128)(2,1)S(1)}, bf16[2,256,512]{2,1,0:T(8,128)(2,1)S(1)}, u32[]{:S(2)}, u32[]{:S(2)}) %collective-permute-start.55) | collective-permute-done | bytes 524320 | tf_op jit(solution)/shard_map/ppermute | solution.py:46
  207.6 1.6 collective-permute-done.49
  210.7 2.8 %collective-permute-done.38.p3 = bf16[2,64,512]{2,1,0:T(8,128)(2,1)S(1)} collective-permute-done((bf16[2,64,512]{2,1,0:T(8,128)(2,1)S(1)}, bf16[2,64,512]{2,1,0:T(8,128)(2,1)S(1)}, u32[]{:S(2)}, u32[]{:S(2)}) %collective-permute-start.38) | collective-permute-done | bytes 131104 | tf_op jit(solution)/shard_map/ppermute | solution.py:46
  215.5 2.9 %shard_map.197 = (f32[256,4,512]{2,1,0:T(4,128)}, f32[256,4,512]{2,1,0:T(4,128)}) custom-call(s32[1]{0:T(128)} %bitcast.own_ref.a_0_, bf16[2,256,512]{2,1,0:T(8,128)(2,1)S(1)} %add_convert_fusion.3.refs_0_, bf16[2,256,512]{2,1,0:T(8,128)(2,1)S(1)} %collective-permute-done.54.refs_1_, bf16[2,256,512]{2,1,0:T(8,128)(2,1)S(1)} %collective-permute-done.55.refs_2_, ...), custom_call_target="tpu_custom_call" | custom-call | flops 345001 | bytes 31 | tf_op jit(solution)/shard_map/pallas_call | solution.py:502
  (173 shorter events, 47.7 us)
Async XLA Ops:
  4.2 11.1 %collective-permute-start = (bf16[64,1152]{1,0:T(8,128)(2,1)S(1)}, bf16[64,1152]{1,0:T(8,128)(2,1)S(1)}, u32[]{:S(2)}, u32[]{:S(2)}) collective-permute-start(bf16[64,1152]{1,0:T(8,128)(2,1)S(1)} %shard_map.178), channel_id=1, source_target_pairs={{0,4},{1,5},{2,6},{3,7},{4,0},{5,1},{6,2},{7,3},{8,12},{9,13},{10,... | collective-permute-start | bytes 442376 | tf_op jit(solution)/shard_map/ppermute | solution.py:46
  12.4 8.5 %collective-permute-start.5 = (bf16[2,64,1152]{2,1,0:T(8,128)(2,1)}, bf16[2,64,1152]{2,1,0:T(8,128)(2,1)S(1)}, u32[]{:S(2)}, u32[]{:S(2)}) collective-permute-start(bf16[2,64,1152]{2,1,0:T(8,128)(2,1)} %get-tuple-element.214), channel_id=1, source_target_pairs={{0,8},{8,0},{16,24},{24,16},{1,9},{9,1},{17,25},{25,17},{2,10},{10... | collective-permute-start | bytes 884744 | tf_op jit(solution)/shard_map/ppermute | solution.py:46
  12.4 10.7 %collective-permute-start.6 = (bf16[2,64,1152]{2,1,0:T(8,128)(2,1)S(1)}, bf16[2,64,1152]{2,1,0:T(8,128)(2,1)S(1)}, u32[]{:S(2)}, u32[]{:S(2)}) collective-permute-start(bf16[2,64,1152]{2,1,0:T(8,128)(2,1)S(1)} %get-tuple-element.213), channel_id=1, source_target_pairs={{0,16},{8,24},{16,0},{24,8},{1,17},{9,25},{17,1},{25,9},{2,18},{10... | collective-permute-start | bytes 884744 | tf_op jit(solution)/shard_map/ppermute | solution.py:46
  13.9 13.9 %collective-permute-start.7 = (bf16[2,64,1152]{2,1,0:T(8,128)(2,1)S(1)}, bf16[2,64,1152]{2,1,0:T(8,128)(2,1)S(1)}, u32[]{:S(2)}, u32[]{:S(2)}) collective-permute-start(bf16[2,64,1152]{2,1,0:T(8,128)(2,1)S(1)} %get-tuple-element.212), channel_id=1, source_target_pairs={{0,24},{8,16},{16,8},{24,0},{1,25},{9,17},{17,9},{25,1},{2,26},{10... | collective-permute-start | bytes 884744 | tf_op jit(solution)/shard_map/ppermute | solution.py:46
  15.4 12.7 %collective-permute-start.9 = (bf16[2,64,1152]{2,1,0:T(8,128)(2,1)S(1)}, bf16[2,64,1152]{2,1,0:T(8,128)(2,1)S(1)}, u32[]{:S(2)}, u32[]{:S(2)}) collective-permute-start(bf16[2,64,1152]{2,1,0:T(8,128)(2,1)S(1)} %pad_maximum_fusion.1.a_1_), channel_id=1, source_target_pairs={{2,0},{3,2},{1,3},{0,1},{6,4},{7,6},{5,7},{4,5},{10,8},{11,10},{9,... | collective-permute-start | bytes 884744 | tf_op jit(solution)/shard_map/ppermute | solution.py:46
  17.0 12.7 %collective-permute-start.8 = (bf16[2,64,1152]{2,1,0:T(8,128)(2,1)S(1)}, bf16[2,64,1152]{2,1,0:T(8,128)(2,1)S(1)}, u32[]{:S(2)}, u32[]{:S(2)}) collective-permute-start(bf16[2,64,1152]{2,1,0:T(8,128)(2,1)S(1)} %pad_maximum_fusion.1.a_1_), channel_id=1, source_target_pairs={{0,2},{2,3},{3,1},{1,0},{4,6},{6,7},{7,5},{5,4},{8,10},{10,11},{11... | collective-permute-start | bytes 884744 | tf_op jit(solution)/shard_map/ppermute | solution.py:46
  20.9 25.3 %collective-permute-start.1 = (bf16[2,256,512]{2,1,0:T(8,128)(2,1)S(1)}, bf16[2,256,512]{2,1,0:T(8,128)(2,1)S(1)}, u32[]{:S(2)}, u32[]{:S(2)}) collective-permute-start(bf16[2,256,512]{2,1,0:T(8,128)(2,1)S(1)} %pad_maximum_fusion), channel_id=1, source_target_pairs={{0,4},{1,5},{2,6},{3,7},{4,0},{5,1},{6,2},{7,3},{8,12},{9,13},{10,... | collective-permute-start | bytes 1572872 | tf_op jit(solution)/shard_map/ppermute | solution.py:46
  29.7 7.7 %collective-permute-start.10 = (bf16[1,64,1152]{2,1,0:T(8,128)(2,1)S(1)}, bf16[1,64,1152]{2,1,0:T(8,128)(2,1)S(1)}, u32[]{:S(2)}, u32[]{:S(2)}) collective-permute-start(bf16[1,64,1152]{2,1,0:T(8,128)(2,1)S(1)} %slice.96), channel_id=1, source_target_pairs={{0,2},{2,3},{3,1},{1,0},{4,6},{6,7},{7,5},{5,4},{8,10},{10,11},{11... | collective-permute-start | bytes 442376 | tf_op jit(solution)/shard_map/ppermute | solution.py:46
  39.5 18.8 %collective-permute-start.12 = (bf16[512,1152]{1,0:T(8,128)(2,1)S(1)}, bf16[512,1152]{1,0:T(8,128)(2,1)S(1)}, u32[]{:S(2)}, u32[]{:S(2)}) collective-permute-start(bf16[512,1152]{1,0:T(8,128)(2,1)S(1)} %shard_map.181.mine_ref), channel_id=1, source_target_pairs={{0,8},{8,0},{16,24},{24,16},{1,9},{9,1},{17,25},{25,17},{2,10},{10... | collective-permute-start | bytes 3538952 | tf_op jit(solution)/shard_map/ppermute | solution.py:46
  46.1 12.1 %collective-permute-start.3 = (bf16[2,256,512]{2,1,0:T(8,128)(2,1)S(1)}, bf16[2,256,512]{2,1,0:T(8,128)(2,1)S(1)}, u32[]{:S(2)}, u32[]{:S(2)}) collective-permute-start(bf16[2,256,512]{2,1,0:T(8,128)(2,1)S(1)} %collective-permute-done.1.refs_2_), channel_id=1, source_target_pairs={{0,16},{8,24},{16,0},{24,8},{1,17},{9,25},{17,1},{25,9},{2,18},{10... | collective-permute-start | bytes 1572872 | tf_op jit(solution)/shard_map/ppermute | solution.py:46
  47.6 19.2 %collective-permute-start.17 = (bf16[2,272,512]{2,1,0:T(8,128)(2,1)S(1)}, bf16[2,272,512]{2,1,0:T(8,128)(2,1)S(1)}, u32[]{:S(2)}, u32[]{:S(2)}) collective-permute-start(bf16[2,272,512]{2,1,0:T(8,128)(2,1)S(1)} %get-tuple-element.109.a_7_.a_8_.refs_8_), channel_id=1, source_target_pairs={{0,2},{2,3},{3,1},{1,0},{4,6},{6,7},{7,5},{5,4},{8,10},{10,11},{11... | collective-permute-start | bytes 1671176 | tf_op jit(solution)/shard_map/ppermute | solution.py:46
  48.3 19.6 %collective-permute-start.19 = (bf16[2,272,512]{2,1,0:T(8,128)(2,1)S(1)}, bf16[2,272,512]{2,1,0:T(8,128)(2,1)S(1)}, u32[]{:S(2)}, u32[]{:S(2)}) collective-permute-start(bf16[2,272,512]{2,1,0:T(8,128)(2,1)S(1)} %get-tuple-element.109.a_7_.a_8_.refs_8_), channel_id=1, source_target_pairs={{2,0},{3,2},{1,3},{0,1},{6,4},{7,6},{5,7},{4,5},{10,8},{11,10},{9,... | collective-permute-start | bytes 1671176 | tf_op jit(solution)/shard_map/ppermute | solution.py:46
  49.6 20.3 %collective-permute-start.2 = (bf16[2,256,512]{2,1,0:T(8,128)(2,1)S(1)}, bf16[2,256,512]{2,1,0:T(8,128)(2,1)S(1)}, u32[]{:S(2)}, u32[]{:S(2)}) collective-permute-start(bf16[2,256,512]{2,1,0:T(8,128)(2,1)S(1)} %collective-permute-done.1.refs_2_), channel_id=1, source_target_pairs={{0,8},{8,0},{16,24},{24,16},{1,9},{9,1},{17,25},{25,17},{2,10},{10... | collective-permute-start | bytes 1572872 | tf_op jit(solution)/shard_map/ppermute | solution.py:46
  58.3 11.8 %collective-permute-start.4 = (bf16[2,256,512]{2,1,0:T(8,128)(2,1)S(1)}, bf16[2,256,512]{2,1,0:T(8,128)(2,1)S(1)}, u32[]{:S(2)}, u32[]{:S(2)}) collective-permute-start(bf16[2,256,512]{2,1,0:T(8,128)(2,1)S(1)} %collective-permute-done.3.refs_4_), channel_id=1, source_target_pairs={{0,8},{8,0},{16,24},{24,16},{1,9},{9,1},{17,25},{25,17},{2,10},{10... | collective-permute-start | bytes 1572872 | tf_op jit(solution)/shard_map/ppermute | solution.py:46
  65.3 13.7 %collective-permute-start.15 = (bf16[1,256,512]{2,1,0:T(8,128)(2,1)S(1)}, bf16[1,256,512]{2,1,0:T(8,128)(2,1)S(1)}, u32[]{:S(2)}, u32[]{:S(2)}) collective-permute-start(bf16[1,256,512]{2,1,0:T(8,128)(2,1)S(1)} %get-tuple-element.103.a_6_.refs_7_), channel_id=1, source_target_pairs={{2,0},{3,2},{1,3},{0,1},{6,4},{7,6},{5,7},{4,5},{10,8},{11,10},{9,... | collective-permute-start | bytes 786440 | tf_op jit(solution)/shard_map/ppermute | solution.py:46
  66.8 12.3 %collective-permute-start.13 = (bf16[1,256,512]{2,1,0:T(8,128)(2,1)S(1)}, bf16[1,256,512]{2,1,0:T(8,128)(2,1)S(1)}, u32[]{:S(2)}, u32[]{:S(2)}) collective-permute-start(bf16[1,256,512]{2,1,0:T(8,128)(2,1)S(1)} %get-tuple-element.102.a_5_.refs_6_), channel_id=1, source_target_pairs={{0,2},{2,3},{3,1},{1,0},{4,6},{6,7},{7,5},{5,4},{8,10},{10,11},{11... | collective-permute-start | bytes 786440 | tf_op jit(solution)/shard_map/ppermute | solution.py:46
  67.9 14.1 %collective-permute-start.21 = (bf16[1,256,512]{2,1,0:T(8,128)(2,1)S(1)}, bf16[1,256,512]{2,1,0:T(8,128)(2,1)S(1)}, u32[]{:S(2)}, u32[]{:S(2)}) collective-permute-start(bf16[1,256,512]{2,1,0:T(8,128)(2,1)S(1)} %get-tuple-element.103.a_6_.refs_7_), channel_id=1, source_target_pairs={{0,2},{2,3},{3,1},{1,0},{4,6},{6,7},{7,5},{5,4},{8,10},{10,11},{11... | collective-permute-start | bytes 786440 | tf_op jit(solution)/shard_map/ppermute | solution.py:46
  69.9 22.9 %collective-permute-start.20 = (bf16[1,272,512]{2,1,0:T(8,128)(2,1)S(1)}, bf16[1,272,512]{2,1,0:T(8,128)(2,1)S(1)}, u32[]{:S(2)}, u32[]{:S(2)}) collective-permute-start(bf16[1,272,512]{2,1,0:T(8,128)(2,1)S(1)} %slice.99), channel_id=1, source_target_pairs={{2,0},{3,2},{1,3},{0,1},{6,4},{7,6},{5,7},{4,5},{10,8},{11,10},{9,... | collective-permute-start | bytes 835592 | tf_op jit(solution)/shard_map/ppermute | solution.py:46
  70.1 22.8 %collective-permute-start.18 = (bf16[1,272,512]{2,1,0:T(8,128)(2,1)S(1)}, bf16[1,272,512]{2,1,0:T(8,128)(2,1)S(1)}, u32[]{:S(2)}, u32[]{:S(2)}) collective-permute-start(bf16[1,272,512]{2,1,0:T(8,128)(2,1)S(1)} %slice.98), channel_id=1, source_target_pairs={{0,2},{2,3},{3,1},{1,0},{4,6},{6,7},{7,5},{5,4},{8,10},{10,11},{11... | collective-permute-start | bytes 835592 | tf_op jit(solution)/shard_map/ppermute | solution.py:46
  79.0 9.3 %collective-permute-start.22 = (bf16[1,256,512]{2,1,0:T(8,128)(2,1)S(1)}, bf16[1,256,512]{2,1,0:T(8,128)(2,1)S(1)}, u32[]{:S(2)}, u32[]{:S(2)}) collective-permute-start(bf16[1,256,512]{2,1,0:T(8,128)(2,1)S(1)} %get-tuple-element.102.a_5_.refs_6_), channel_id=1, source_target_pairs={{2,0},{3,2},{1,3},{0,1},{6,4},{7,6},{5,7},{4,5},{10,8},{11,10},{9,... | collective-permute-start | bytes 786440 | tf_op jit(solution)/shard_map/ppermute | solution.py:46
  79.2 13.6 %collective-permute-start.16 = (bf16[1,256,512]{2,1,0:T(8,128)(2,1)S(1)}, bf16[1,256,512]{2,1,0:T(8,128)(2,1)S(1)}, u32[]{:S(2)}, u32[]{:S(2)}) collective-permute-start(bf16[1,256,512]{2,1,0:T(8,128)(2,1)S(1)} %collective-permute-done.15.a_6_), channel_id=1, source_target_pairs={{2,0},{3,2},{1,3},{0,1},{6,4},{7,6},{5,7},{4,5},{10,8},{11,10},{9,... | collective-permute-start | bytes 786440 | tf_op jit(solution)/shard_map/ppermute | solution.py:46
  82.0 11.2 %collective-permute-start.14 = (bf16[1,256,512]{2,1,0:T(8,128)(2,1)S(1)}, bf16[1,256,512]{2,1,0:T(8,128)(2,1)S(1)}, u32[]{:S(2)}, u32[]{:S(2)}) collective-permute-start(bf16[1,256,512]{2,1,0:T(8,128)(2,1)S(1)} %collective-permute-done.13.a_5_), channel_id=1, source_target_pairs={{0,2},{2,3},{3,1},{1,0},{4,6},{6,7},{7,5},{5,4},{8,10},{10,11},{11... | collective-permute-start | bytes 786440 | tf_op jit(solution)/shard_map/ppermute | solution.py:46
  100.5 13.5 %collective-permute-start.23 = (bf16[2,2,256,512]{3,2,1,0:T(8,128)(2,1)S(1)}, bf16[2,2,256,512]{3,2,1,0:T(8,128)(2,1)S(1)}, u32[]{:S(2)}, u32[]{:S(2)}) collective-permute-start(bf16[2,2,256,512]{3,2,1,0:T(8,128)(2,1)S(1)} %shard_map.187), channel_id=1, source_target_pairs={{0,8},{8,0},{16,24},{24,16},{1,9},{9,1},{17,25},{25,17},{2,10},{10... | collective-permute-start | bytes 3145736 | tf_op jit(solution)/shard_map/ppermute | solution.py:46
  100.6 10.5 %collective-permute-start.25 = (bf16[1,528,256]{2,1,0:T(8,128)(2,1)S(1)}, bf16[1,528,256]{2,1,0:T(8,128)(2,1)S(1)}, u32[]{:S(2)}, u32[]{:S(2)}) collective-permute-start(bf16[1,528,256]{2,1,0:T(8,128)(2,1)S(1)} %get-tuple-element.134), channel_id=1, source_target_pairs={{2,0},{3,2},{1,3},{0,1},{6,4},{7,6},{5,7},{4,5},{10,8},{11,10},{9,... | collective-permute-start | bytes 811016 | tf_op jit(solution)/shard_map/ppermute | solution.py:46
  102.3 9.3 %collective-permute-start.24 = (bf16[1,528,256]{2,1,0:T(8,128)(2,1)S(1)}, bf16[1,528,256]{2,1,0:T(8,128)(2,1)S(1)}, u32[]{:S(2)}, u32[]{:S(2)}) collective-permute-start(bf16[1,528,256]{2,1,0:T(8,128)(2,1)S(1)} %get-tuple-element.130), channel_id=1, source_target_pairs={{0,2},{2,3},{3,1},{1,0},{4,6},{6,7},{7,5},{5,4},{8,10},{10,11},{11... | collective-permute-start | bytes 811016 | tf_op jit(solution)/shard_map/ppermute | solution.py:46
  102.6 23.6 %collective-permute-start.27 = (bf16[1,528,256]{2,1,0:T(8,128)(2,1)S(1)}, bf16[1,528,256]{2,1,0:T(8,128)(2,1)S(1)}, u32[]{:S(2)}, u32[]{:S(2)}) collective-permute-start(bf16[1,528,256]{2,1,0:T(8,128)(2,1)S(1)} %get-tuple-element.138), channel_id=1, source_target_pairs={{0,2},{2,3},{3,1},{1,0},{4,6},{6,7},{7,5},{5,4},{8,10},{10,11},{11... | collective-permute-start | bytes 811016 | tf_op jit(solution)/shard_map/ppermute | solution.py:46
  103.8 22.5 %collective-permute-start.28 = (bf16[1,528,256]{2,1,0:T(8,128)(2,1)S(1)}, bf16[1,528,256]{2,1,0:T(8,128)(2,1)S(1)}, u32[]{:S(2)}, u32[]{:S(2)}) collective-permute-start(bf16[1,528,256]{2,1,0:T(8,128)(2,1)S(1)} %get-tuple-element.139), channel_id=1, source_target_pairs={{2,0},{3,2},{1,3},{0,1},{6,4},{7,6},{5,7},{4,5},{10,8},{11,10},{9,... | collective-permute-start | bytes 811016 | tf_op jit(solution)/shard_map/ppermute | solution.py:46
  111.8 14.5 %collective-permute-start.29 = (bf16[1,528,256]{2,1,0:T(8,128)(2,1)S(1)}, bf16[1,528,256]{2,1,0:T(8,128)(2,1)S(1)}, u32[]{:S(2)}, u32[]{:S(2)}) collective-permute-start(bf16[1,528,256]{2,1,0:T(8,128)(2,1)S(1)} %add_convert_fusion.4), channel_id=1, source_target_pairs={{2,0},{3,2},{1,3},{0,1},{6,4},{7,6},{5,7},{4,5},{10,8},{11,10},{9,... | collective-permute-start | bytes 811016 | tf_op jit(solution)/shard_map/ppermute | solution.py:46
  113.0 13.2 %collective-permute-start.26 = (bf16[1,528,256]{2,1,0:T(8,128)(2,1)S(1)}, bf16[1,528,256]{2,1,0:T(8,128)(2,1)S(1)}, u32[]{:S(2)}, u32[]{:S(2)}) collective-permute-start(bf16[1,528,256]{2,1,0:T(8,128)(2,1)S(1)} %add_convert_fusion.5), channel_id=1, source_target_pairs={{0,2},{2,3},{3,1},{1,0},{4,6},{6,7},{7,5},{5,4},{8,10},{10,11},{11... | collective-permute-start | bytes 811016 | tf_op jit(solution)/shard_map/ppermute | solution.py:46
  115.1 30.6 %collective-permute-start.39 = (bf16[2,256,512]{2,1,0:T(8,128)(2,1)S(1)}, bf16[2,256,512]{2,1,0:T(8,128)(2,1)}, u32[]{:S(2)}, u32[]{:S(2)}) collective-permute-start(bf16[2,256,512]{2,1,0:T(8,128)(2,1)S(1)} %get-tuple-element.217), channel_id=1, source_target_pairs={{0,16},{8,24},{16,0},{24,8},{1,17},{9,25},{17,1},{25,9},{2,18},{10... | collective-permute-start | bytes 1572872 | tf_op jit(solution)/shard_map/ppermute | solution.py:46
  127.1 18.6 %collective-permute-start.30 = (bf16[1,512,256]{2,1,0:T(8,128)(2,1)S(1)}, bf16[1,512,256]{2,1,0:T(8,128)(2,1)S(1)}, u32[]{:S(2)}, u32[]{:S(2)}) collective-permute-start(bf16[1,512,256]{2,1,0:T(8,128)(2,1)S(1)} %get-tuple-element.205), channel_id=1, source_target_pairs={{0,2},{2,3},{3,1},{1,0},{4,6},{6,7},{7,5},{5,4},{8,10},{10,11},{11... | collective-permute-start | bytes 786440 | tf_op jit(solution)/shard_map/ppermute | solution.py:46
  127.7 18.1 %collective-permute-start.34 = (bf16[1,512,256]{2,1,0:T(8,128)(2,1)S(1)}, bf16[1,512,256]{2,1,0:T(8,128)(2,1)S(1)}, u32[]{:S(2)}, u32[]{:S(2)}) collective-permute-start(bf16[1,512,256]{2,1,0:T(8,128)(2,1)S(1)} %get-tuple-element.202), channel_id=1, source_target_pairs={{2,0},{3,2},{1,3},{0,1},{6,4},{7,6},{5,7},{4,5},{10,8},{11,10},{9,... | collective-permute-start | bytes 786440 | tf_op jit(solution)/shard_map/ppermute | solution.py:46
  147.0 18.9 %collective-permute-start.52 = (bf16[2,256,512]{2,1,0:T(8,128)(2,1)}, bf16[2,256,512]{2,1,0:T(8,128)(2,1)S(1)}, u32[]{:S(2)}, u32[]{:S(2)}) collective-permute-start(bf16[2,256,512]{2,1,0:T(8,128)(2,1)} %get-tuple-element.216), channel_id=1, source_target_pairs={{0,16},{8,24},{16,0},{24,8},{1,17},{9,25},{17,1},{25,9},{2,18},{10... | collective-permute-start | bytes 1572872 | tf_op jit(solution)/shard_map/ppermute | solution.py:46
  147.6 49.8 %collective-permute-start.32 = (bf16[1,512,256]{2,1,0:T(8,128)(2,1)}, bf16[1,512,256]{2,1,0:T(8,128)(2,1)S(1)}, u32[]{:S(2)}, u32[]{:S(2)}) collective-permute-start(bf16[1,512,256]{2,1,0:T(8,128)(2,1)} %get-tuple-element.204), channel_id=1, source_target_pairs={{0,2},{2,3},{3,1},{1,0},{4,6},{6,7},{7,5},{5,4},{8,10},{10,11},{11... | collective-permute-start | bytes 786440 | tf_op jit(solution)/shard_map/ppermute | solution.py:46
  159.0 14.4 %collective-permute-start.47 = (bf16[2,64,1152]{2,1,0:T(8,128)(2,1)S(1)}, bf16[2,64,1152]{2,1,0:T(8,128)(2,1)S(1)}, u32[]{:S(2)}, u32[]{:S(2)}) collective-permute-start(bf16[2,64,1152]{2,1,0:T(8,128)(2,1)S(1)} %pad_maximum_fusion.3), channel_id=1, source_target_pairs={{2,0},{3,2},{1,3},{0,1},{6,4},{7,6},{5,7},{4,5},{10,8},{11,10},{9,... | collective-permute-start | bytes 884744 | tf_op jit(solution)/shard_map/ppermute | solution.py:46
  160.3 13.2 %collective-permute-start.42 = (bf16[2,64,1152]{2,1,0:T(8,128)(2,1)S(1)}, bf16[2,64,1152]{2,1,0:T(8,128)(2,1)S(1)}, u32[]{:S(2)}, u32[]{:S(2)}) collective-permute-start(bf16[2,64,1152]{2,1,0:T(8,128)(2,1)S(1)} %pad_maximum_fusion.2), channel_id=1, source_target_pairs={{0,2},{2,3},{3,1},{1,0},{4,6},{6,7},{7,5},{5,4},{8,10},{10,11},{11... | collective-permute-start | bytes 884744 | tf_op jit(solution)/shard_map/ppermute | solution.py:46
  162.4 25.4 %collective-permute-start.53 = (bf16[2,256,512]{2,1,0:T(8,128)(2,1)S(1)}, bf16[2,256,512]{2,1,0:T(8,128)(2,1)S(1)}, u32[]{:S(2)}, u32[]{:S(2)}) collective-permute-start(bf16[2,256,512]{2,1,0:T(8,128)(2,1)S(1)} %fusion.4), channel_id=1, source_target_pairs={{0,4},{1,5},{2,6},{3,7},{4,0},{5,1},{6,2},{7,3},{8,12},{9,13},{10,... | collective-permute-start | bytes 1572872 | tf_op jit(solution)/shard_map/ppermute | solution.py:46
  166.0 32.2 %collective-permute-start.33 = (bf16[1,512,256]{2,1,0:T(8,128)(2,1)S(1)}, bf16[1,512,256]{2,1,0:T(8,128)(2,1)S(1)}, u32[]{:S(2)}, u32[]{:S(2)}) collective-permute-start(bf16[1,512,256]{2,1,0:T(8,128)(2,1)S(1)} %copy-done.21), channel_id=1, source_target_pairs={{2,0},{3,2},{1,3},{0,1},{6,4},{7,6},{5,7},{4,5},{10,8},{11,10},{9,... | collective-permute-start | bytes 786440 | tf_op jit(solution)/shard_map/ppermute | solution.py:46
  173.5 24.8 %collective-permute-start.31 = (bf16[1,512,256]{2,1,0:T(8,128)(2,1)S(1)}, bf16[1,512,256]{2,1,0:T(8,128)(2,1)S(1)}, u32[]{:S(2)}, u32[]{:S(2)}) collective-permute-start(bf16[1,512,256]{2,1,0:T(8,128)(2,1)S(1)} %get-tuple-element.201), channel_id=1, source_target_pairs={{0,2},{2,3},{3,1},{1,0},{4,6},{6,7},{7,5},{5,4},{8,10},{10,11},{11... | collective-permute-start | bytes 786440 | tf_op jit(solution)/shard_map/ppermute | solution.py:46
  173.5 24.8 %collective-permute-start.35 = (bf16[1,512,256]{2,1,0:T(8,128)(2,1)S(1)}, bf16[1,512,256]{2,1,0:T(8,128)(2,1)S(1)}, u32[]{:S(2)}, u32[]{:S(2)}) collective-permute-start(bf16[1,512,256]{2,1,0:T(8,128)(2,1)S(1)} %get-tuple-element.200), channel_id=1, source_target_pairs={{2,0},{3,2},{1,3},{0,1},{6,4},{7,6},{5,7},{4,5},{10,8},{11,10},{9,... | collective-permute-start | bytes 786440 | tf_op jit(solution)/shard_map/ppermute | solution.py:46
  187.7 8.3 %collective-permute-start.48 = (bf16[1,64,1152]{2,1,0:T(8,128)(2,1)S(1)}, bf16[1,64,1152]{2,1,0:T(8,128)(2,1)S(1)}, u32[]{:S(2)}, u32[]{:S(2)}) collective-permute-start(bf16[1,64,1152]{2,1,0:T(8,128)(2,1)S(1)} %fusion.7), channel_id=1, source_target_pairs={{0,4},{1,5},{2,6},{3,7},{4,0},{5,1},{6,2},{7,3},{8,12},{9,13},{10,... | collective-permute-start | bytes 442376 | tf_op jit(solution)/shard_map/ppermute | solution.py:46
  196.0 11.6 %collective-permute-start.55 = (bf16[2,256,512]{2,1,0:T(8,128)(2,1)S(1)}, bf16[2,256,512]{2,1,0:T(8,128)(2,1)S(1)}, u32[]{:S(2)}, u32[]{:S(2)}) collective-permute-start(bf16[2,256,512]{2,1,0:T(8,128)(2,1)S(1)} %add_convert_fusion.3.refs_0_), channel_id=1, source_target_pairs={{0,16},{8,24},{16,0},{24,8},{1,17},{9,25},{17,1},{25,9},{2,18},{10... | collective-permute-start | bytes 1572872 | tf_op jit(solution)/shard_map/ppermute | solution.py:46
  197.3 11.9 %collective-permute-start.49 = (bf16[64,1152]{1,0:T(8,128)(2,1)S(1)}, bf16[64,1152]{1,0:T(8,128)(2,1)S(1)}, u32[]{:S(2)}, u32[]{:S(2)}) collective-permute-start(bf16[64,1152]{1,0:T(8,128)(2,1)S(1)} %fusion.15), channel_id=1, source_target_pairs={{0,16},{8,24},{16,0},{24,8},{1,17},{9,25},{17,1},{25,9},{2,18},{10... | collective-permute-start | bytes 442376 | tf_op jit(solution)/shard_map/ppermute | solution.py:46
  198.2 16.4 %collective-permute-start.54 = (bf16[2,256,512]{2,1,0:T(8,128)(2,1)S(1)}, bf16[2,256,512]{2,1,0:T(8,128)(2,1)S(1)}, u32[]{:S(2)}, u32[]{:S(2)}) collective-permute-start(bf16[2,256,512]{2,1,0:T(8,128)(2,1)S(1)} %add_convert_fusion.3.refs_0_), channel_id=1, source_target_pairs={{0,8},{8,0},{16,24},{24,16},{1,9},{9,1},{17,25},{25,17},{2,10},{10... | collective-permute-start | bytes 1572872 | tf_op jit(solution)/shard_map/ppermute | solution.py:46
  199.1 10.2 %collective-permute-start.36 = (bf16[2,64,512]{2,1,0:T(8,128)(2,1)S(1)}, bf16[2,64,512]{2,1,0:T(8,128)(2,1)S(1)}, u32[]{:S(2)}, u32[]{:S(2)}) collective-permute-start(bf16[2,64,512]{2,1,0:T(8,128)(2,1)S(1)} %get-tuple-element.151), channel_id=1, source_target_pairs={{0,8},{8,0},{16,24},{24,16},{1,9},{9,1},{17,25},{25,17},{2,10},{10... | collective-permute-start | bytes 393224 | tf_op jit(solution)/shard_map/ppermute | solution.py:46
  199.6 11.0 %collective-permute-start.37 = (bf16[2,64,512]{2,1,0:T(8,128)(2,1)S(1)}, bf16[2,64,512]{2,1,0:T(8,128)(2,1)S(1)}, u32[]{:S(2)}, u32[]{:S(2)}) collective-permute-start(bf16[2,64,512]{2,1,0:T(8,128)(2,1)S(1)} %get-tuple-element.152), channel_id=1, source_target_pairs={{0,16},{8,24},{16,0},{24,8},{1,17},{9,25},{17,1},{25,9},{2,18},{10... | collective-permute-start | bytes 393224 | tf_op jit(solution)/shard_map/ppermute | solution.py:46
  209.3 10.8 %collective-permute-start.50 = (bf16[64,1152]{1,0:T(8,128)(2,1)S(1)}, bf16[64,1152]{1,0:T(8,128)(2,1)S(1)}, u32[]{:S(2)}, u32[]{:S(2)}) collective-permute-start(bf16[64,1152]{1,0:T(8,128)(2,1)S(1)} %add_convert_fusion.8.mine_ref), channel_id=1, source_target_pairs={{0,8},{8,0},{16,24},{24,16},{1,9},{9,1},{17,25},{25,17},{2,10},{10... | collective-permute-start | bytes 442376 | tf_op jit(solution)/shard_map/ppermute | solution.py:46
  210.6 7.7 %collective-permute-start.45 = (bf16[2,64,512]{2,1,0:T(8,128)(2,1)S(1)}, bf16[2,64,512]{2,1,0:T(8,128)(2,1)S(1)}, u32[]{:S(2)}, u32[]{:S(2)}) collective-permute-start(bf16[2,64,512]{2,1,0:T(8,128)(2,1)S(1)} %copy-done.14), channel_id=1, source_target_pairs={{0,24},{8,16},{16,8},{24,0},{1,25},{9,17},{17,9},{25,1},{2,26},{10... | collective-permute-start | bytes 393224 | tf_op jit(solution)/shard_map/ppermute | solution.py:46
  (31 other events, 225.5 us)
where the time goes:
time: 224 us; the launch traced here: 222 us
  waiting for transfers between devices  75.7 us (34%)
  Pallas kernels  67.2 us (30%)
  starting transfers between devices  52.9 us (24%)
  local copies, waits for them, and re-layouts  16.4 us (7%)
  other arithmetic  8.89 us (4%)
    ppermute x57, waiting for transfers between devices, send(): return lax.ppermute(x, axis, pairs)  75.7 us
    ppermute x57, starting transfers between devices, send(): return lax.ppermute(x, axis, pairs)  52.9 us
    pallas_call x4, Pallas kernels, moe_call(): pl.pallas_call(lambda *a: moe_kernel(starts, len(aliased), *a), grid=(tot...  17.8 us
    pallas_call x1, Pallas kernels, attn_bwd(): pl.pallas_call(attn_bwd_kernel, grid_spec=pltpu.PrefetchScalarGridSpec(nu...  14.2 us
    pallas_call x4, Pallas kernels, moe_grad(): pl.pallas_call(lambda *a: moe_grad_kernel(groups, *a), grid=(2, groups),...  12 us
    unnamed x49, local copies, waits for them, and re-layouts  7.68 us
    pallas_call x1, Pallas kernels, attn_fwd(): pl.pallas_call(attn_fwd_kernel, grid_spec=pltpu.PrefetchScalarGridSpec(nu...  7.03 us
    pallas_call x1, Pallas kernels, moe_out(): pl.pallas_call(moe_out_kernel, grid=(units,), in_specs=[pl.BlockSpec((wid...  5.77 us
  transfers between devices with their start and end apart: 57, of which 20 were waited for; matrix products, arithmetic and copies ran while one was open for 7% of the time, Pallas kernels for 27%

commit v1 on v0

--- a/solution.py
+++ b/solution.py
@@ -932,7 +932,7 @@
         dx_ahead, dx_behind, far, fw4, bw4, lambda a: after(a, grad1), seen
     )
     kept2 = add_low(grad2, send(grad3, "seq", by_core))
-    grad0 = moe_grad(after(ga, kept2, *seen), hg, xb, gb, 0)
+    grad0 = moe_grad(after(ga, *seen), hg, xb, gb, 0)
     kept0 = add_low(grad0, send(grad1, "seq", by_core))
     outs = moe_out(woutt, after(ga, grad0))
     first_half = send(kept2[1], "seq", by_half)

time: 224 us -> 224 us (level)
  no operation moved by 1% of the time
where the time goes in v1:
time: 224 us; the launch traced here: 222 us
  waiting for transfers between devices  77.1 us (34%)
  Pallas kernels  67.2 us (30%)
  starting transfers between devices  51.6 us (23%)
  local copies, waits for them, and re-layouts  16.4 us (7%)
  other arithmetic  8.8 us (4%)
    ppermute x57, waiting for transfers between devices, send(): return lax.ppermute(x, axis, pairs)  77.1 us
    ppermute x57, starting transfers between devices, send(): return lax.ppermute(x, axis, pairs)  51.6 us
    pallas_call x4, Pallas kernels, moe_call(): pl.pallas_call(lambda *a: moe_kernel(starts, len(aliased), *a), grid=(tot...  17.8 us
    pallas_call x1, Pallas kernels, attn_bwd(): pl.pallas_call(attn_bwd_kernel, grid_spec=pltpu.PrefetchScalarGridSpec(nu...  14.2 us
    pallas_call x4, Pallas kernels, moe_grad(): pl.pallas_call(lambda *a: moe_grad_kernel(groups, *a), grid=(2, groups),...  12 us
    unnamed x49, local copies, waits for them, and re-layouts  7.68 us
    pallas_call x1, Pallas kernels, attn_fwd(): pl.pallas_call(attn_fwd_kernel, grid_spec=pltpu.PrefetchScalarGridSpec(nu...  7.03 us
    pallas_call x1, Pallas kernels, moe_out(): pl.pallas_call(moe_out_kernel, grid=(units,), in_specs=[pl.BlockSpec((wid...  5.77 us
  transfers between devices with their start and end apart: 57, of which 20 were waited for; matrix products, arithmetic and copies ran while one was open for 7% of the time, Pallas kernels for 27%

profile of v1, /device:TPU:0, one launch (start us, length us, event | category | flops | bytes accessed | tf_op | source)
XLA Modules:
  0.0 222.4 jit_solution(8915157464269620016)
XLA Ops:
  4.2 4.1 %collective-permute-start = (bf16[64,1152]{1,0:T(8,128)(2,1)S(1)}, bf16[64,1152]{1,0:T(8,128)(2,1)S(1)}, u32[]{:S(2)}, u32[]{:S(2)}) collective-permute-start(bf16[64,1152]{1,0:T(8,128)(2,1)S(1)} %shard_map.178), channel_id=1, source_target_pairs={{0,4},{1,5},{2,6},{3,7},{4,0},{5,1},{6,2},{7,3},{8,12},{9,13},{10,... | collective-permute-start | bytes 442376 | tf_op jit(solution)/shard_map/ppermute | solution.py:46
  12.4 1.5 collective-permute-start.6
  15.4 1.6 collective-permute-start.9
  17.4 3.2 %constant_dynamic-slice_fusion = (bf16[256,1,512]{2,1,0:T(2,128)(2,1)S(1)}, bf16[256,1,512]{2,1,0:T(2,128)(2,1)S(1)}) fusion(f32[256,4,512]{2,1,0:T(4,128)} %param.20, s32[]{:T(128)S(6)} %select_n.90, f32[256,4,512]{2,1,0:T(4,128)} %param.19), kind=kLoop, calls=%fused_computation.60 | loop fusion | bytes 1048580 | tf_op jit(solution)/shard_map/jit(dynamic_index_in_dim)/dynamic_slice | solution.py:842
  20.9 2.2 collective-permute-start.1
  23.1 4.6 %collective-permute-done.7.p3 = bf16[2,64,1152]{2,1,0:T(8,128)(2,1)S(1)} collective-permute-done((bf16[2,64,1152]{2,1,0:T(8,128)(2,1)S(1)}, bf16[2,64,1152]{2,1,0:T(8,128)(2,1)S(1)}, u32[]{:S(2)}, u32[]{:S(2)}) %collective-permute-start.7) | collective-permute-done | bytes 294944 | tf_op jit(solution)/shard_map/ppermute | solution.py:46
  28.1 1.6 collective-permute-start.11
  30.2 4.2 %collective-permute-done.11.a_5_ = bf16[1,64,1152]{2,1,0:T(8,128)(2,1)S(1)} collective-permute-done((bf16[1,64,1152]{2,1,0:T(8,128)(2,1)S(1)}, bf16[1,64,1152]{2,1,0:T(8,128)(2,1)S(1)}, u32[]{:S(2)}, u32[]{:S(2)}) %collective-permute-start.11) | collective-permute-done | bytes 147488 | tf_op jit(solution)/shard_map/ppermute | solution.py:46
  34.4 3.0 %collective-permute-done.10.a_4_ = bf16[1,64,1152]{2,1,0:T(8,128)(2,1)S(1)} collective-permute-done((bf16[1,64,1152]{2,1,0:T(8,128)(2,1)S(1)}, bf16[1,64,1152]{2,1,0:T(8,128)(2,1)S(1)}, u32[]{:S(2)}, u32[]{:S(2)}) %collective-permute-start.10) | collective-permute-done | bytes 147488 | tf_op jit(solution)/shard_map/ppermute | solution.py:46
  37.4 2.2 shard_map.181.mine_ref
  39.6 6.5 %collective-permute-done.1.refs_2_ = bf16[2,256,512]{2,1,0:T(8,128)(2,1)S(1)} collective-permute-done((bf16[2,256,512]{2,1,0:T(8,128)(2,1)S(1)}, bf16[2,256,512]{2,1,0:T(8,128)(2,1)S(1)}, u32[]{:S(2)}, u32[]{:S(2)}) %collective-permute-start.1) | collective-permute-done | bytes 524320 | tf_op jit(solution)/shard_map/ppermute | solution.py:46
  46.1 1.5 collective-permute-start.3
  49.7 8.6 %collective-permute-done.3.refs_4_ = bf16[2,256,512]{2,1,0:T(8,128)(2,1)S(1)} collective-permute-done((bf16[2,256,512]{2,1,0:T(8,128)(2,1)S(1)}, bf16[2,256,512]{2,1,0:T(8,128)(2,1)S(1)}, u32[]{:S(2)}, u32[]{:S(2)}) %collective-permute-start.3) | collective-permute-done | bytes 524320 | tf_op jit(solution)/shard_map/ppermute | solution.py:46
  58.3 7.0 %shard_map.182 = (bf16[1,256,512]{2,1,0:T(8,128)(2,1)S(1)}, bf16[1,256,512]{2,1,0:T(8,128)(2,1)S(1)}, f32[2,256,512]{2,1,0:T(8,128)S(1)}, bf16[2,256,1536]{2,1,0...) custom-call(s32[1]{0:T(128)} %bitcast.own_ref.a_0_, ...), custom_call_target="tpu_custom_call" | custom-call | flops 920001 | bytes 81 | tf_op jit(solution)/shard_map/pallas_call | solution.py:225
  65.3 1.5 collective-permute-start.15
  67.9 1.9 collective-permute-start.21
  70.1 1.9 collective-permute-start.18
  74.5 4.5 %shard_map.183 = (bf16[1,528,256]{2,1,0:T(8,128)(2,1)S(1)}, bf16[1,528,256]{2,1,0:T(8,128)(2,1)S(1)}, bf16[8,2048,256]{2,1,0:T(8,128)(2,1)S(1)}, bf16[8,2048,256...) custom-call(s32[1]{0:T(128)} %bitcast.own_ref.a_0_, ...), custom_call_target="tpu_custom_call" | custom-call | flops 598001 | bytes 53 | tf_op jit(solution)/shard_map/pallas_call | solution.py:383
  79.2 1.4 collective-permute-start.16
  80.6 1.4 collective-permute-done.21.a_5_
  82.6 4.5 %shard_map.184 = (bf16[1,528,256]{2,1,0:T(8,128)(2,1)S(1)}, bf16[1,528,256]{2,1,0:T(8,128)(2,1)S(1)}, bf16[8,2048,256]{2,1,0:T(8,128)(2,1)S(1)}, bf16[8,2048,256...) custom-call(s32[1]{0:T(128)} %bitcast.own_ref.a_0_, ...), custom_call_target="tpu_custom_call", output_to_operand_aliasing={{2}: (9, {}), {3}: (10, {}), {4}: (11, {}), {5}: (12, {})} | custom-call | flops 598001 | bytes 53 | tf_op jit(solution)/shard_map/pallas_call | solution.py:383
  88.3 4.5 %shard_map.185 = (bf16[1,528,256]{2,1,0:T(8,128)(2,1)S(1)}, bf16[1,528,256]{2,1,0:T(8,128)(2,1)S(1)}, bf16[8,2048,256]{2,1,0:T(8,128)(2,1)S(1)}, bf16[8,2048,256...) custom-call(s32[1]{0:T(128)} %bitcast.own_ref.a_0_, ...), custom_call_target="tpu_custom_call", output_to_operand_aliasing={{2}: (9, {}), {3}: (10, {}), {4}: (11, {}), {5}: (12, {})} | custom-call | flops 598001 | bytes 53 | tf_op jit(solution)/shard_map/pallas_call | solution.py:383
  93.2 4.4 %shard_map.186 = (bf16[1,528,256]{2,1,0:T(8,128)(2,1)S(1)}, bf16[1,528,256]{2,1,0:T(8,128)(2,1)S(1)}, bf16[8,2048,256]{2,1,0:T(8,128)(2,1)S(1)}, bf16[8,2048,256...) custom-call(s32[1]{0:T(128)} %bitcast.own_ref.a_0_, ...), custom_call_target="tpu_custom_call", output_to_operand_aliasing={{2}: (9, {}), {3}: (10, {}), {4}: (11, {}), {5}: (12, {})} | custom-call | flops 598001 | bytes 53 | tf_op jit(solution)/shard_map/pallas_call | solution.py:383
  97.6 2.8 %shard_map.187 = bf16[2,2,256,512]{3,2,1,0:T(8,128)(2,1)S(1)} custom-call(bf16[8,2048,256]{2,1,0:T(8,128)(2,1)S(1)} %get-tuple-element.137.a_0_.ga_ref, bf16[8,2048,256]{2,1,0:T(8,128)(2,1)S(1)} %get-tuple-element.127.a_1_, bf16[8,256,512]{2,1,0:T(8,128)(2,1)S(1)} %get-tuple-element.128.a_2_, bf16[8,272,512]{2,1,0:T(8,128)(2,1)S(1)} %get-tuple-element.129.a_3_), custom_call_target="tpu_custom_call" | custom-call | flops 432401 | bytes 38 | tf_op jit(solution)/shard_map/pallas_call | solution.py:469
  100.6 1.8 collective-permute-start.24
  104.7 2.8 %shard_map.188 = bf16[2,2,256,512]{3,2,1,0:T(8,128)(2,1)S(1)} custom-call(bf16[8,2048,256]{2,1,0:T(8,128)(2,1)S(1)} %get-tuple-element.137.a_0_.ga_ref, bf16[8,2048,256]{2,1,0:T(8,128)(2,1)S(1)} %get-tuple-element.127.a_1_, bf16[8,256,512]{2,1,0:T(8,128)(2,1)S(1)} %get-tuple-element.128.a_2_, bf16[8,272,512]{2,1,0:T(8,128)(2,1)S(1)} %get-tuple-element.129.a_3_), custom_call_target="tpu_custom_call" | custom-call | flops 432401 | bytes 38 | tf_op jit(solution)/shard_map/pallas_call | solution.py:469
  107.5 3.6 %shard_map.189 = bf16[2,2,256,512]{3,2,1,0:T(8,128)(2,1)} custom-call(bf16[8,2048,256]{2,1,0:T(8,128)(2,1)S(1)} %get-tuple-element.137.a_0_.ga_ref, bf16[8,2048,256]{2,1,0:T(8,128)(2,1)S(1)} %get-tuple-element.127.a_1_, bf16[8,256,512]{2,1,0:T(8,128)(2,1)S(1)} %get-tuple-element.128.a_2_, bf16[8,272,512]{2,1,0:T(8,128)(2,1)S(1)} %get-tuple-element.129.a_3_), custom_call_target="tpu_custom_call" | custom-call | flops 432401 | bytes 38 | tf_op jit(solution)/shard_map/pallas_call | solution.py:469
  115.1 1.5 collective-permute-start.39
  116.6 2.8 %shard_map.190 = bf16[2,2,256,512]{3,2,1,0:T(8,128)(2,1)S(1)} custom-call(bf16[8,2048,256]{2,1,0:T(8,128)(2,1)S(1)} %get-tuple-element.137.a_0_.ga_ref, bf16[8,2048,256]{2,1,0:T(8,128)(2,1)S(1)} %get-tuple-element.127.a_1_, bf16[8,256,512]{2,1,0:T(8,128)(2,1)S(1)} %get-tuple-element.128.a_2_, bf16[8,272,512]{2,1,0:T(8,128)(2,1)S(1)} %get-tuple-element.129.a_3_), custom_call_target="tpu_custom_call" | custom-call | flops 432401 | bytes 38 | tf_op jit(solution)/shard_map/pallas_call | solution.py:469
  120.4 5.8 %shard_map.191.refs_0_ = bf16[8,512,256]{2,1,0:T(8,128)(2,1)S(1)} custom-call(bf16[512,2048]{1,0:T(8,128)(2,1)S(1)} %get-tuple-element.93.woutt_ref, bf16[8,2048,256]{2,1,0:T(8,128)(2,1)S(1)} %get-tuple-element.137.a_0_.ga_ref), custom_call_target="tpu_custom_call" | custom-call | flops 644001 | bytes 57 | tf_op jit(solution)/shard_map/pallas_call | solution.py:420
  127.7 1.5 collective-permute-start.33
  129.2 14.2 %shard_map.192 = (bf16[2,64,512]{2,1,0:T(8,128)(2,1)S(1)}, bf16[2,64,512]{2,1,0:T(8,128)(2,1)S(1)}, bf16[2,64,512]{2,1,0:T(8,128)(2,1)S(1)}, bf16[2,64,512]{2,1,...) custom-call(s32[1]{0:T(128)} %bitcast.own_ref.a_0_, ...), custom_call_target="tpu_custom_call" | custom-call | flops 1955001 | bytes 171 | tf_op jit(solution)/shard_map/pallas_call | solution.py:630
  148.1 1.6 collective-permute-done.40
  149.7 1.9 add_convert_fusion
  152.3 1.5 collective-permute-start.46
  153.8 1.5 add_convert_fusion.1
  155.3 3.3 %collective-permute-done.41 = bf16[1,64,1152]{2,1,0:T(8,128)(2,1)S(1)} collective-permute-done((bf16[1,64,1152]{2,1,0:T(8,128)(2,1)S(1)}, bf16[1,64,1152]{2,1,0:T(8,128)(2,1)S(1)}, u32[]{:S(2)}, u32[]{:S(2)}) %collective-permute-start.41) | collective-permute-done | bytes 147488 | tf_op jit(solution)/shard_map/ppermute | solution.py:46
  162.1 3.4 %collective-permute-start.53 = (bf16[2,256,512]{2,1,0:T(8,128)(2,1)S(1)}, bf16[2,256,512]{2,1,0:T(8,128)(2,1)S(1)}, u32[]{:S(2)}, u32[]{:S(2)}) collective-permute-start(bf16[2,256,512]{2,1,0:T(8,128)(2,1)S(1)} %fusion.4), channel_id=1, source_target_pairs={{0,4},{1,5},{2,6},{3,7},{4,0},{5,1},{6,2},{7,3},{8,12},{9,13},{10,... | collective-permute-start | bytes 1572872 | tf_op jit(solution)/shard_map/ppermute | solution.py:46
  166.9 6.4 %collective-permute-done.47 = bf16[2,64,1152]{2,1,0:T(8,128)(2,1)S(1)} collective-permute-done((bf16[2,64,1152]{2,1,0:T(8,128)(2,1)S(1)}, bf16[2,64,1152]{2,1,0:T(8,128)(2,1)S(1)}, u32[]{:S(2)}, u32[]{:S(2)}) %collective-permute-start.47) | collective-permute-done | bytes 294944 | tf_op jit(solution)/shard_map/ppermute | solution.py:46
  173.3 2.3 %collective-permute-start.34 = (bf16[1,512,256]{2,1,0:T(8,128)(2,1)S(1)}, bf16[1,512,256]{2,1,0:T(8,128)(2,1)S(1)}, u32[]{:S(2)}, u32[]{:S(2)}) collective-permute-start(bf16[1,512,256]{2,1,0:T(8,128)(2,1)S(1)} %get-tuple-element.200), channel_id=1, source_target_pairs={{2,0},{3,2},{1,3},{0,1},{6,4},{7,6},{5,7},{4,5},{10,8},{11,10},{9,... | collective-permute-start | bytes 786440 | tf_op jit(solution)/shard_map/ppermute | solution.py:46
  175.7 11.9 %collective-permute-done.53 = bf16[2,256,512]{2,1,0:T(8,128)(2,1)S(1)} collective-permute-done((bf16[2,256,512]{2,1,0:T(8,128)(2,1)S(1)}, bf16[2,256,512]{2,1,0:T(8,128)(2,1)S(1)}, u32[]{:S(2)}, u32[]{:S(2)}) %collective-permute-start.53) | collective-permute-done | bytes 524320 | tf_op jit(solution)/shard_map/ppermute | solution.py:46
  187.8 8.1 %collective-permute-done.48 = bf16[1,64,1152]{2,1,0:T(8,128)(2,1)S(1)} collective-permute-done((bf16[1,64,1152]{2,1,0:T(8,128)(2,1)S(1)}, bf16[1,64,1152]{2,1,0:T(8,128)(2,1)S(1)}, u32[]{:S(2)}, u32[]{:S(2)}) %collective-permute-start.48) | collective-permute-done | bytes 147488 | tf_op jit(solution)/shard_map/ppermute | solution.py:46
  196.6 1.6 collective-permute-start.49
  200.1 7.5 %collective-permute-done.55.refs_2_ = bf16[2,256,512]{2,1,0:T(8,128)(2,1)S(1)} collective-permute-done((bf16[2,256,512]{2,1,0:T(8,128)(2,1)S(1)}, bf16[2,256,512]{2,1,0:T(8,128)(2,1)S(1)}, u32[]{:S(2)}, u32[]{:S(2)}) %collective-permute-start.55) | collective-permute-done | bytes 524320 | tf_op jit(solution)/shard_map/ppermute | solution.py:46
  207.6 1.6 collective-permute-done.49
  210.6 2.9 %collective-permute-done.37.p3 = bf16[2,64,512]{2,1,0:T(8,128)(2,1)S(1)} collective-permute-done((bf16[2,64,512]{2,1,0:T(8,128)(2,1)S(1)}, bf16[2,64,512]{2,1,0:T(8,128)(2,1)S(1)}, u32[]{:S(2)}, u32[]{:S(2)}) %collective-permute-start.37) | collective-permute-done | bytes 131104 | tf_op jit(solution)/shard_map/ppermute | solution.py:46
  214.8 2.9 %shard_map.197 = (f32[256,4,512]{2,1,0:T(4,128)}, f32[256,4,512]{2,1,0:T(4,128)}) custom-call(s32[1]{0:T(128)} %bitcast.own_ref.a_0_, bf16[2,256,512]{2,1,0:T(8,128)(2,1)S(1)} %add_convert_fusion.3.refs_0_, bf16[2,256,512]{2,1,0:T(8,128)(2,1)S(1)} %collective-permute-done.54.refs_1_, bf16[2,256,512]{2,1,0:T(8,128)(2,1)S(1)} %collective-permute-done.55.refs_2_, ...), custom_call_target="tpu_custom_call" | custom-call | flops 345001 | bytes 31 | tf_op jit(solution)/shard_map/pallas_call | solution.py:502
  217.6 1.4 collective-permute-done.44.p2
  (173 shorter events, 46.7 us)
Async XLA Ops:
  4.2 11.1 %collective-permute-start = (bf16[64,1152]{1,0:T(8,128)(2,1)S(1)}, bf16[64,1152]{1,0:T(8,128)(2,1)S(1)}, u32[]{:S(2)}, u32[]{:S(2)}) collective-permute-start(bf16[64,1152]{1,0:T(8,128)(2,1)S(1)} %shard_map.178), channel_id=1, source_target_pairs={{0,4},{1,5},{2,6},{3,7},{4,0},{5,1},{6,2},{7,3},{8,12},{9,13},{10,... | collective-permute-start | bytes 442376 | tf_op jit(solution)/shard_map/ppermute | solution.py:46
  12.4 8.5 %collective-permute-start.5 = (bf16[2,64,1152]{2,1,0:T(8,128)(2,1)}, bf16[2,64,1152]{2,1,0:T(8,128)(2,1)S(1)}, u32[]{:S(2)}, u32[]{:S(2)}) collective-permute-start(bf16[2,64,1152]{2,1,0:T(8,128)(2,1)} %get-tuple-element.214), channel_id=1, source_target_pairs={{0,8},{8,0},{16,24},{24,16},{1,9},{9,1},{17,25},{25,17},{2,10},{10... | collective-permute-start | bytes 884744 | tf_op jit(solution)/shard_map/ppermute | solution.py:46
  12.4 10.7 %collective-permute-start.6 = (bf16[2,64,1152]{2,1,0:T(8,128)(2,1)S(1)}, bf16[2,64,1152]{2,1,0:T(8,128)(2,1)S(1)}, u32[]{:S(2)}, u32[]{:S(2)}) collective-permute-start(bf16[2,64,1152]{2,1,0:T(8,128)(2,1)S(1)} %get-tuple-element.213), channel_id=1, source_target_pairs={{0,16},{8,24},{16,0},{24,8},{1,17},{9,25},{17,1},{25,9},{2,18},{10... | collective-permute-start | bytes 884744 | tf_op jit(solution)/shard_map/ppermute | solution.py:46
  13.9 13.9 %collective-permute-start.7 = (bf16[2,64,1152]{2,1,0:T(8,128)(2,1)S(1)}, bf16[2,64,1152]{2,1,0:T(8,128)(2,1)S(1)}, u32[]{:S(2)}, u32[]{:S(2)}) collective-permute-start(bf16[2,64,1152]{2,1,0:T(8,128)(2,1)S(1)} %get-tuple-element.212), channel_id=1, source_target_pairs={{0,24},{8,16},{16,8},{24,0},{1,25},{9,17},{17,9},{25,1},{2,26},{10... | collective-permute-start | bytes 884744 | tf_op jit(solution)/shard_map/ppermute | solution.py:46
  15.4 12.7 %collective-permute-start.9 = (bf16[2,64,1152]{2,1,0:T(8,128)(2,1)S(1)}, bf16[2,64,1152]{2,1,0:T(8,128)(2,1)S(1)}, u32[]{:S(2)}, u32[]{:S(2)}) collective-permute-start(bf16[2,64,1152]{2,1,0:T(8,128)(2,1)S(1)} %pad_maximum_fusion.1.a_1_), channel_id=1, source_target_pairs={{2,0},{3,2},{1,3},{0,1},{6,4},{7,6},{5,7},{4,5},{10,8},{11,10},{9,... | collective-permute-start | bytes 884744 | tf_op jit(solution)/shard_map/ppermute | solution.py:46
  17.0 12.7 %collective-permute-start.8 = (bf16[2,64,1152]{2,1,0:T(8,128)(2,1)S(1)}, bf16[2,64,1152]{2,1,0:T(8,128)(2,1)S(1)}, u32[]{:S(2)}, u32[]{:S(2)}) collective-permute-start(bf16[2,64,1152]{2,1,0:T(8,128)(2,1)S(1)} %pad_maximum_fusion.1.a_1_), channel_id=1, source_target_pairs={{0,2},{2,3},{3,1},{1,0},{4,6},{6,7},{7,5},{5,4},{8,10},{10,11},{11... | collective-permute-start | bytes 884744 | tf_op jit(solution)/shard_map/ppermute | solution.py:46
  20.9 25.3 %collective-permute-start.1 = (bf16[2,256,512]{2,1,0:T(8,128)(2,1)S(1)}, bf16[2,256,512]{2,1,0:T(8,128)(2,1)S(1)}, u32[]{:S(2)}, u32[]{:S(2)}) collective-permute-start(bf16[2,256,512]{2,1,0:T(8,128)(2,1)S(1)} %pad_maximum_fusion), channel_id=1, source_target_pairs={{0,4},{1,5},{2,6},{3,7},{4,0},{5,1},{6,2},{7,3},{8,12},{9,13},{10,... | collective-permute-start | bytes 1572872 | tf_op jit(solution)/shard_map/ppermute | solution.py:46
  29.7 7.7 %collective-permute-start.10 = (bf16[1,64,1152]{2,1,0:T(8,128)(2,1)S(1)}, bf16[1,64,1152]{2,1,0:T(8,128)(2,1)S(1)}, u32[]{:S(2)}, u32[]{:S(2)}) collective-permute-start(bf16[1,64,1152]{2,1,0:T(8,128)(2,1)S(1)} %slice.96), channel_id=1, source_target_pairs={{0,2},{2,3},{3,1},{1,0},{4,6},{6,7},{7,5},{5,4},{8,10},{10,11},{11... | collective-permute-start | bytes 442376 | tf_op jit(solution)/shard_map/ppermute | solution.py:46
  39.5 18.8 %collective-permute-start.12 = (bf16[512,1152]{1,0:T(8,128)(2,1)S(1)}, bf16[512,1152]{1,0:T(8,128)(2,1)S(1)}, u32[]{:S(2)}, u32[]{:S(2)}) collective-permute-start(bf16[512,1152]{1,0:T(8,128)(2,1)S(1)} %shard_map.181.mine_ref), channel_id=1, source_target_pairs={{0,8},{8,0},{16,24},{24,16},{1,9},{9,1},{17,25},{25,17},{2,10},{10... | collective-permute-start | bytes 3538952 | tf_op jit(solution)/shard_map/ppermute | solution.py:46
  46.1 12.1 %collective-permute-start.3 = (bf16[2,256,512]{2,1,0:T(8,128)(2,1)S(1)}, bf16[2,256,512]{2,1,0:T(8,128)(2,1)S(1)}, u32[]{:S(2)}, u32[]{:S(2)}) collective-permute-start(bf16[2,256,512]{2,1,0:T(8,128)(2,1)S(1)} %collective-permute-done.1.refs_2_), channel_id=1, source_target_pairs={{0,16},{8,24},{16,0},{24,8},{1,17},{9,25},{17,1},{25,9},{2,18},{10... | collective-permute-start | bytes 1572872 | tf_op jit(solution)/shard_map/ppermute | solution.py:46
  47.6 19.2 %collective-permute-start.17 = (bf16[2,272,512]{2,1,0:T(8,128)(2,1)S(1)}, bf16[2,272,512]{2,1,0:T(8,128)(2,1)S(1)}, u32[]{:S(2)}, u32[]{:S(2)}) collective-permute-start(bf16[2,272,512]{2,1,0:T(8,128)(2,1)S(1)} %get-tuple-element.109.a_7_.a_8_.refs_8_), channel_id=1, source_target_pairs={{0,2},{2,3},{3,1},{1,0},{4,6},{6,7},{7,5},{5,4},{8,10},{10,11},{11... | collective-permute-start | bytes 1671176 | tf_op jit(solution)/shard_map/ppermute | solution.py:46
  48.3 19.6 %collective-permute-start.19 = (bf16[2,272,512]{2,1,0:T(8,128)(2,1)S(1)}, bf16[2,272,512]{2,1,0:T(8,128)(2,1)S(1)}, u32[]{:S(2)}, u32[]{:S(2)}) collective-permute-start(bf16[2,272,512]{2,1,0:T(8,128)(2,1)S(1)} %get-tuple-element.109.a_7_.a_8_.refs_8_), channel_id=1, source_target_pairs={{2,0},{3,2},{1,3},{0,1},{6,4},{7,6},{5,7},{4,5},{10,8},{11,10},{9,... | collective-permute-start | bytes 1671176 | tf_op jit(solution)/shard_map/ppermute | solution.py:46
  49.6 20.3 %collective-permute-start.2 = (bf16[2,256,512]{2,1,0:T(8,128)(2,1)S(1)}, bf16[2,256,512]{2,1,0:T(8,128)(2,1)S(1)}, u32[]{:S(2)}, u32[]{:S(2)}) collective-permute-start(bf16[2,256,512]{2,1,0:T(8,128)(2,1)S(1)} %collective-permute-done.1.refs_2_), channel_id=1, source_target_pairs={{0,8},{8,0},{16,24},{24,16},{1,9},{9,1},{17,25},{25,17},{2,10},{10... | collective-permute-start | bytes 1572872 | tf_op jit(solution)/shard_map/ppermute | solution.py:46
  58.3 11.8 %collective-permute-start.4 = (bf16[2,256,512]{2,1,0:T(8,128)(2,1)S(1)}, bf16[2,256,512]{2,1,0:T(8,128)(2,1)S(1)}, u32[]{:S(2)}, u32[]{:S(2)}) collective-permute-start(bf16[2,256,512]{2,1,0:T(8,128)(2,1)S(1)} %collective-permute-done.3.refs_4_), channel_id=1, source_target_pairs={{0,8},{8,0},{16,24},{24,16},{1,9},{9,1},{17,25},{25,17},{2,10},{10... | collective-permute-start | bytes 1572872 | tf_op jit(solution)/shard_map/ppermute | solution.py:46
  65.3 13.7 %collective-permute-start.15 = (bf16[1,256,512]{2,1,0:T(8,128)(2,1)S(1)}, bf16[1,256,512]{2,1,0:T(8,128)(2,1)S(1)}, u32[]{:S(2)}, u32[]{:S(2)}) collective-permute-start(bf16[1,256,512]{2,1,0:T(8,128)(2,1)S(1)} %get-tuple-element.103.a_6_.refs_7_), channel_id=1, source_target_pairs={{2,0},{3,2},{1,3},{0,1},{6,4},{7,6},{5,7},{4,5},{10,8},{11,10},{9,... | collective-permute-start | bytes 786440 | tf_op jit(solution)/shard_map/ppermute | solution.py:46
  66.8 12.3 %collective-permute-start.13 = (bf16[1,256,512]{2,1,0:T(8,128)(2,1)S(1)}, bf16[1,256,512]{2,1,0:T(8,128)(2,1)S(1)}, u32[]{:S(2)}, u32[]{:S(2)}) collective-permute-start(bf16[1,256,512]{2,1,0:T(8,128)(2,1)S(1)} %get-tuple-element.102.a_5_.refs_6_), channel_id=1, source_target_pairs={{0,2},{2,3},{3,1},{1,0},{4,6},{6,7},{7,5},{5,4},{8,10},{10,11},{11... | collective-permute-start | bytes 786440 | tf_op jit(solution)/shard_map/ppermute | solution.py:46
  67.9 14.1 %collective-permute-start.21 = (bf16[1,256,512]{2,1,0:T(8,128)(2,1)S(1)}, bf16[1,256,512]{2,1,0:T(8,128)(2,1)S(1)}, u32[]{:S(2)}, u32[]{:S(2)}) collective-permute-start(bf16[1,256,512]{2,1,0:T(8,128)(2,1)S(1)} %get-tuple-element.103.a_6_.refs_7_), channel_id=1, source_target_pairs={{0,2},{2,3},{3,1},{1,0},{4,6},{6,7},{7,5},{5,4},{8,10},{10,11},{11... | collective-permute-start | bytes 786440 | tf_op jit(solution)/shard_map/ppermute | solution.py:46
  69.9 22.9 %collective-permute-start.20 = (bf16[1,272,512]{2,1,0:T(8,128)(2,1)S(1)}, bf16[1,272,512]{2,1,0:T(8,128)(2,1)S(1)}, u32[]{:S(2)}, u32[]{:S(2)}) collective-permute-start(bf16[1,272,512]{2,1,0:T(8,128)(2,1)S(1)} %slice.99), channel_id=1, source_target_pairs={{2,0},{3,2},{1,3},{0,1},{6,4},{7,6},{5,7},{4,5},{10,8},{11,10},{9,... | collective-permute-start | bytes 835592 | tf_op jit(solution)/shard_map/ppermute | solution.py:46
  70.1 22.8 %collective-permute-start.18 = (bf16[1,272,512]{2,1,0:T(8,128)(2,1)S(1)}, bf16[1,272,512]{2,1,0:T(8,128)(2,1)S(1)}, u32[]{:S(2)}, u32[]{:S(2)}) collective-permute-start(bf16[1,272,512]{2,1,0:T(8,128)(2,1)S(1)} %slice.98), channel_id=1, source_target_pairs={{0,2},{2,3},{3,1},{1,0},{4,6},{6,7},{7,5},{5,4},{8,10},{10,11},{11... | collective-permute-start | bytes 835592 | tf_op jit(solution)/shard_map/ppermute | solution.py:46
  79.0 9.3 %collective-permute-start.22 = (bf16[1,256,512]{2,1,0:T(8,128)(2,1)S(1)}, bf16[1,256,512]{2,1,0:T(8,128)(2,1)S(1)}, u32[]{:S(2)}, u32[]{:S(2)}) collective-permute-start(bf16[1,256,512]{2,1,0:T(8,128)(2,1)S(1)} %get-tuple-element.102.a_5_.refs_6_), channel_id=1, source_target_pairs={{2,0},{3,2},{1,3},{0,1},{6,4},{7,6},{5,7},{4,5},{10,8},{11,10},{9,... | collective-permute-start | bytes 786440 | tf_op jit(solution)/shard_map/ppermute | solution.py:46
  79.2 13.6 %collective-permute-start.16 = (bf16[1,256,512]{2,1,0:T(8,128)(2,1)S(1)}, bf16[1,256,512]{2,1,0:T(8,128)(2,1)S(1)}, u32[]{:S(2)}, u32[]{:S(2)}) collective-permute-start(bf16[1,256,512]{2,1,0:T(8,128)(2,1)S(1)} %collective-permute-done.15.a_6_), channel_id=1, source_target_pairs={{2,0},{3,2},{1,3},{0,1},{6,4},{7,6},{5,7},{4,5},{10,8},{11,10},{9,... | collective-permute-start | bytes 786440 | tf_op jit(solution)/shard_map/ppermute | solution.py:46
  82.0 11.2 %collective-permute-start.14 = (bf16[1,256,512]{2,1,0:T(8,128)(2,1)S(1)}, bf16[1,256,512]{2,1,0:T(8,128)(2,1)S(1)}, u32[]{:S(2)}, u32[]{:S(2)}) collective-permute-start(bf16[1,256,512]{2,1,0:T(8,128)(2,1)S(1)} %collective-permute-done.13.a_5_), channel_id=1, source_target_pairs={{0,2},{2,3},{3,1},{1,0},{4,6},{6,7},{7,5},{5,4},{8,10},{10,11},{11... | collective-permute-start | bytes 786440 | tf_op jit(solution)/shard_map/ppermute | solution.py:46
  100.5 13.5 %collective-permute-start.38 = (bf16[2,2,256,512]{3,2,1,0:T(8,128)(2,1)S(1)}, bf16[2,2,256,512]{3,2,1,0:T(8,128)(2,1)S(1)}, u32[]{:S(2)}, u32[]{:S(2)}) collective-permute-start(bf16[2,2,256,512]{3,2,1,0:T(8,128)(2,1)S(1)} %shard_map.187), channel_id=1, source_target_pairs={{0,8},{8,0},{16,24},{24,16},{1,9},{9,1},{17,25},{25,17},{2,10},{10... | collective-permute-start | bytes 3145736 | tf_op jit(solution)/shard_map/ppermute | solution.py:46
  100.6 10.5 %collective-permute-start.24 = (bf16[1,528,256]{2,1,0:T(8,128)(2,1)S(1)}, bf16[1,528,256]{2,1,0:T(8,128)(2,1)S(1)}, u32[]{:S(2)}, u32[]{:S(2)}) collective-permute-start(bf16[1,528,256]{2,1,0:T(8,128)(2,1)S(1)} %get-tuple-element.134), channel_id=1, source_target_pairs={{2,0},{3,2},{1,3},{0,1},{6,4},{7,6},{5,7},{4,5},{10,8},{11,10},{9,... | collective-permute-start | bytes 811016 | tf_op jit(solution)/shard_map/ppermute | solution.py:46
  102.3 9.3 %collective-permute-start.23 = (bf16[1,528,256]{2,1,0:T(8,128)(2,1)S(1)}, bf16[1,528,256]{2,1,0:T(8,128)(2,1)S(1)}, u32[]{:S(2)}, u32[]{:S(2)}) collective-permute-start(bf16[1,528,256]{2,1,0:T(8,128)(2,1)S(1)} %get-tuple-element.126), channel_id=1, source_target_pairs={{0,2},{2,3},{3,1},{1,0},{4,6},{6,7},{7,5},{5,4},{8,10},{10,11},{11... | collective-permute-start | bytes 811016 | tf_op jit(solution)/shard_map/ppermute | solution.py:46
  102.6 23.6 %collective-permute-start.26 = (bf16[1,528,256]{2,1,0:T(8,128)(2,1)S(1)}, bf16[1,528,256]{2,1,0:T(8,128)(2,1)S(1)}, u32[]{:S(2)}, u32[]{:S(2)}) collective-permute-start(bf16[1,528,256]{2,1,0:T(8,128)(2,1)S(1)} %get-tuple-element.138), channel_id=1, source_target_pairs={{0,2},{2,3},{3,1},{1,0},{4,6},{6,7},{7,5},{5,4},{8,10},{10,11},{11... | collective-permute-start | bytes 811016 | tf_op jit(solution)/shard_map/ppermute | solution.py:46
  103.8 22.5 %collective-permute-start.27 = (bf16[1,528,256]{2,1,0:T(8,128)(2,1)S(1)}, bf16[1,528,256]{2,1,0:T(8,128)(2,1)S(1)}, u32[]{:S(2)}, u32[]{:S(2)}) collective-permute-start(bf16[1,528,256]{2,1,0:T(8,128)(2,1)S(1)} %get-tuple-element.139), channel_id=1, source_target_pairs={{2,0},{3,2},{1,3},{0,1},{6,4},{7,6},{5,7},{4,5},{10,8},{11,10},{9,... | collective-permute-start | bytes 811016 | tf_op jit(solution)/shard_map/ppermute | solution.py:46
  111.8 14.5 %collective-permute-start.28 = (bf16[1,528,256]{2,1,0:T(8,128)(2,1)S(1)}, bf16[1,528,256]{2,1,0:T(8,128)(2,1)S(1)}, u32[]{:S(2)}, u32[]{:S(2)}) collective-permute-start(bf16[1,528,256]{2,1,0:T(8,128)(2,1)S(1)} %add_convert_fusion.4), channel_id=1, source_target_pairs={{2,0},{3,2},{1,3},{0,1},{6,4},{7,6},{5,7},{4,5},{10,8},{11,10},{9,... | collective-permute-start | bytes 811016 | tf_op jit(solution)/shard_map/ppermute | solution.py:46
  113.0 13.2 %collective-permute-start.25 = (bf16[1,528,256]{2,1,0:T(8,128)(2,1)S(1)}, bf16[1,528,256]{2,1,0:T(8,128)(2,1)S(1)}, u32[]{:S(2)}, u32[]{:S(2)}) collective-permute-start(bf16[1,528,256]{2,1,0:T(8,128)(2,1)S(1)} %add_convert_fusion.5), channel_id=1, source_target_pairs={{0,2},{2,3},{3,1},{1,0},{4,6},{6,7},{7,5},{5,4},{8,10},{10,11},{11... | collective-permute-start | bytes 811016 | tf_op jit(solution)/shard_map/ppermute | solution.py:46
  115.1 30.6 %collective-permute-start.39 = (bf16[2,256,512]{2,1,0:T(8,128)(2,1)S(1)}, bf16[2,256,512]{2,1,0:T(8,128)(2,1)}, u32[]{:S(2)}, u32[]{:S(2)}) collective-permute-start(bf16[2,256,512]{2,1,0:T(8,128)(2,1)S(1)} %get-tuple-element.217), channel_id=1, source_target_pairs={{0,16},{8,24},{16,0},{24,8},{1,17},{9,25},{17,1},{25,9},{2,18},{10... | collective-permute-start | bytes 1572872 | tf_op jit(solution)/shard_map/ppermute | solution.py:46
  127.1 18.6 %collective-permute-start.29 = (bf16[1,512,256]{2,1,0:T(8,128)(2,1)S(1)}, bf16[1,512,256]{2,1,0:T(8,128)(2,1)S(1)}, u32[]{:S(2)}, u32[]{:S(2)}) collective-permute-start(bf16[1,512,256]{2,1,0:T(8,128)(2,1)S(1)} %get-tuple-element.205), channel_id=1, source_target_pairs={{0,2},{2,3},{3,1},{1,0},{4,6},{6,7},{7,5},{5,4},{8,10},{10,11},{11... | collective-permute-start | bytes 786440 | tf_op jit(solution)/shard_map/ppermute | solution.py:46
  127.7 18.1 %collective-permute-start.33 = (bf16[1,512,256]{2,1,0:T(8,128)(2,1)S(1)}, bf16[1,512,256]{2,1,0:T(8,128)(2,1)S(1)}, u32[]{:S(2)}, u32[]{:S(2)}) collective-permute-start(bf16[1,512,256]{2,1,0:T(8,128)(2,1)S(1)} %get-tuple-element.202), channel_id=1, source_target_pairs={{2,0},{3,2},{1,3},{0,1},{6,4},{7,6},{5,7},{4,5},{10,8},{11,10},{9,... | collective-permute-start | bytes 786440 | tf_op jit(solution)/shard_map/ppermute | solution.py:46
  146.5 7.2 %collective-permute-start.51 = (bf16[2,2,256,512]{3,2,1,0:T(8,128)(2,1)}, bf16[2,2,256,512]{3,2,1,0:T(8,128)(2,1)}, u32[]{:S(2)}, u32[]{:S(2)}) collective-permute-start(bf16[2,2,256,512]{3,2,1,0:T(8,128)(2,1)} %shard_map.189), channel_id=1, source_target_pairs={{0,8},{8,0},{16,24},{24,16},{1,9},{9,1},{17,25},{25,17},{2,10},{10... | collective-permute-start | bytes 3145736 | tf_op jit(solution)/shard_map/ppermute | solution.py:46
  147.0 49.5 %collective-permute-start.31 = (bf16[1,512,256]{2,1,0:T(8,128)(2,1)}, bf16[1,512,256]{2,1,0:T(8,128)(2,1)S(1)}, u32[]{:S(2)}, u32[]{:S(2)}) collective-permute-start(bf16[1,512,256]{2,1,0:T(8,128)(2,1)} %get-tuple-element.204), channel_id=1, source_target_pairs={{0,2},{2,3},{3,1},{1,0},{4,6},{6,7},{7,5},{5,4},{8,10},{10,11},{11... | collective-permute-start | bytes 786440 | tf_op jit(solution)/shard_map/ppermute | solution.py:46
  147.6 18.1 %collective-permute-start.52 = (bf16[2,256,512]{2,1,0:T(8,128)(2,1)}, bf16[2,256,512]{2,1,0:T(8,128)(2,1)S(1)}, u32[]{:S(2)}, u32[]{:S(2)}) collective-permute-start(bf16[2,256,512]{2,1,0:T(8,128)(2,1)} %get-tuple-element.216), channel_id=1, source_target_pairs={{0,16},{8,24},{16,0},{24,8},{1,17},{9,25},{17,1},{25,9},{2,18},{10... | collective-permute-start | bytes 1572872 | tf_op jit(solution)/shard_map/ppermute | solution.py:46
  158.8 14.6 %collective-permute-start.47 = (bf16[2,64,1152]{2,1,0:T(8,128)(2,1)S(1)}, bf16[2,64,1152]{2,1,0:T(8,128)(2,1)S(1)}, u32[]{:S(2)}, u32[]{:S(2)}) collective-permute-start(bf16[2,64,1152]{2,1,0:T(8,128)(2,1)S(1)} %pad_maximum_fusion.3), channel_id=1, source_target_pairs={{2,0},{3,2},{1,3},{0,1},{6,4},{7,6},{5,7},{4,5},{10,8},{11,10},{9,... | collective-permute-start | bytes 884744 | tf_op jit(solution)/shard_map/ppermute | solution.py:46
  160.0 13.3 %collective-permute-start.42 = (bf16[2,64,1152]{2,1,0:T(8,128)(2,1)S(1)}, bf16[2,64,1152]{2,1,0:T(8,128)(2,1)S(1)}, u32[]{:S(2)}, u32[]{:S(2)}) collective-permute-start(bf16[2,64,1152]{2,1,0:T(8,128)(2,1)S(1)} %pad_maximum_fusion.2), channel_id=1, source_target_pairs={{0,2},{2,3},{3,1},{1,0},{4,6},{6,7},{7,5},{5,4},{8,10},{10,11},{11... | collective-permute-start | bytes 884744 | tf_op jit(solution)/shard_map/ppermute | solution.py:46
  162.1 25.5 %collective-permute-start.53 = (bf16[2,256,512]{2,1,0:T(8,128)(2,1)S(1)}, bf16[2,256,512]{2,1,0:T(8,128)(2,1)S(1)}, u32[]{:S(2)}, u32[]{:S(2)}) collective-permute-start(bf16[2,256,512]{2,1,0:T(8,128)(2,1)S(1)} %fusion.4), channel_id=1, source_target_pairs={{0,4},{1,5},{2,6},{3,7},{4,0},{5,1},{6,2},{7,3},{8,12},{9,13},{10,... | collective-permute-start | bytes 1572872 | tf_op jit(solution)/shard_map/ppermute | solution.py:46
  165.7 32.4 %collective-permute-start.32 = (bf16[1,512,256]{2,1,0:T(8,128)(2,1)S(1)}, bf16[1,512,256]{2,1,0:T(8,128)(2,1)S(1)}, u32[]{:S(2)}, u32[]{:S(2)}) collective-permute-start(bf16[1,512,256]{2,1,0:T(8,128)(2,1)S(1)} %copy-done.21), channel_id=1, source_target_pairs={{2,0},{3,2},{1,3},{0,1},{6,4},{7,6},{5,7},{4,5},{10,8},{11,10},{9,... | collective-permute-start | bytes 786440 | tf_op jit(solution)/shard_map/ppermute | solution.py:46
  173.3 24.8 %collective-permute-start.30 = (bf16[1,512,256]{2,1,0:T(8,128)(2,1)S(1)}, bf16[1,512,256]{2,1,0:T(8,128)(2,1)S(1)}, u32[]{:S(2)}, u32[]{:S(2)}) collective-permute-start(bf16[1,512,256]{2,1,0:T(8,128)(2,1)S(1)} %get-tuple-element.201), channel_id=1, source_target_pairs={{0,2},{2,3},{3,1},{1,0},{4,6},{6,7},{7,5},{5,4},{8,10},{10,11},{11... | collective-permute-start | bytes 786440 | tf_op jit(solution)/shard_map/ppermute | solution.py:46
  173.3 24.8 %collective-permute-start.34 = (bf16[1,512,256]{2,1,0:T(8,128)(2,1)S(1)}, bf16[1,512,256]{2,1,0:T(8,128)(2,1)S(1)}, u32[]{:S(2)}, u32[]{:S(2)}) collective-permute-start(bf16[1,512,256]{2,1,0:T(8,128)(2,1)S(1)} %get-tuple-element.200), channel_id=1, source_target_pairs={{2,0},{3,2},{1,3},{0,1},{6,4},{7,6},{5,7},{4,5},{10,8},{11,10},{9,... | collective-permute-start | bytes 786440 | tf_op jit(solution)/shard_map/ppermute | solution.py:46
  187.6 8.3 %collective-permute-start.48 = (bf16[1,64,1152]{2,1,0:T(8,128)(2,1)S(1)}, bf16[1,64,1152]{2,1,0:T(8,128)(2,1)S(1)}, u32[]{:S(2)}, u32[]{:S(2)}) collective-permute-start(bf16[1,64,1152]{2,1,0:T(8,128)(2,1)S(1)} %fusion.7), channel_id=1, source_target_pairs={{0,4},{1,5},{2,6},{3,7},{4,0},{5,1},{6,2},{7,3},{8,12},{9,13},{10,... | collective-permute-start | bytes 442376 | tf_op jit(solution)/shard_map/ppermute | solution.py:46
  195.9 11.7 %collective-permute-start.55 = (bf16[2,256,512]{2,1,0:T(8,128)(2,1)S(1)}, bf16[2,256,512]{2,1,0:T(8,128)(2,1)S(1)}, u32[]{:S(2)}, u32[]{:S(2)}) collective-permute-start(bf16[2,256,512]{2,1,0:T(8,128)(2,1)S(1)} %add_convert_fusion.3.refs_0_), channel_id=1, source_target_pairs={{0,16},{8,24},{16,0},{24,8},{1,17},{9,25},{17,1},{25,9},{2,18},{10... | collective-permute-start | bytes 1572872 | tf_op jit(solution)/shard_map/ppermute | solution.py:46
  196.6 12.6 %collective-permute-start.49 = (bf16[64,1152]{1,0:T(8,128)(2,1)S(1)}, bf16[64,1152]{1,0:T(8,128)(2,1)S(1)}, u32[]{:S(2)}, u32[]{:S(2)}) collective-permute-start(bf16[64,1152]{1,0:T(8,128)(2,1)S(1)} %fusion.15), channel_id=1, source_target_pairs={{0,16},{8,24},{16,0},{24,8},{1,17},{9,25},{17,1},{25,9},{2,18},{10... | collective-permute-start | bytes 442376 | tf_op jit(solution)/shard_map/ppermute | solution.py:46
  198.2 15.8 %collective-permute-start.54 = (bf16[2,256,512]{2,1,0:T(8,128)(2,1)S(1)}, bf16[2,256,512]{2,1,0:T(8,128)(2,1)S(1)}, u32[]{:S(2)}, u32[]{:S(2)}) collective-permute-start(bf16[2,256,512]{2,1,0:T(8,128)(2,1)S(1)} %add_convert_fusion.3.refs_0_), channel_id=1, source_target_pairs={{0,8},{8,0},{16,24},{24,16},{1,9},{9,1},{17,25},{25,17},{2,10},{10... | collective-permute-start | bytes 1572872 | tf_op jit(solution)/shard_map/ppermute | solution.py:46
  199.0 10.2 %collective-permute-start.35 = (bf16[2,64,512]{2,1,0:T(8,128)(2,1)S(1)}, bf16[2,64,512]{2,1,0:T(8,128)(2,1)S(1)}, u32[]{:S(2)}, u32[]{:S(2)}) collective-permute-start(bf16[2,64,512]{2,1,0:T(8,128)(2,1)S(1)} %get-tuple-element.151), channel_id=1, source_target_pairs={{0,8},{8,0},{16,24},{24,16},{1,9},{9,1},{17,25},{25,17},{2,10},{10... | collective-permute-start | bytes 393224 | tf_op jit(solution)/shard_map/ppermute | solution.py:46
  199.6 11.1 %collective-permute-start.36 = (bf16[2,64,512]{2,1,0:T(8,128)(2,1)S(1)}, bf16[2,64,512]{2,1,0:T(8,128)(2,1)S(1)}, u32[]{:S(2)}, u32[]{:S(2)}) collective-permute-start(bf16[2,64,512]{2,1,0:T(8,128)(2,1)S(1)} %get-tuple-element.152), channel_id=1, source_target_pairs={{0,16},{8,24},{16,0},{24,8},{1,17},{9,25},{17,1},{25,9},{2,18},{10... | collective-permute-start | bytes 393224 | tf_op jit(solution)/shard_map/ppermute | solution.py:46
  209.3 10.8 %collective-permute-start.50 = (bf16[64,1152]{1,0:T(8,128)(2,1)S(1)}, bf16[64,1152]{1,0:T(8,128)(2,1)S(1)}, u32[]{:S(2)}, u32[]{:S(2)}) collective-permute-start(bf16[64,1152]{1,0:T(8,128)(2,1)S(1)} %add_convert_fusion.8.mine_ref), channel_id=1, source_target_pairs={{0,8},{8,0},{16,24},{24,16},{1,9},{9,1},{17,25},{25,17},{2,10},{10... | collective-permute-start | bytes 442376 | tf_op jit(solution)/shard_map/ppermute | solution.py:46
  (31 other events, 228.0 us)
